TPU v7x, 32 devices: a whole 2x2x4 slice. The times are simulated.
32 devices in a mesh: mom: 2 (over x), pts: 16 (over z, y, core).
Axes of the slice: x: 2, y: 2, z: 4, core: 2. Of those that a mesh axis runs over, the one named last changes fastest.
Arguments:
- amplitudes: bfloat16 [2, 2, 1, 256, 64, 128], P(None, None, None, 'mom'), may hold values from -6 to 6
- val_orbitals: bfloat16 [2, 256, 64, 512], P(None, 'mom'), may hold values from -0.25 to 0.25
- cond_orbitals: bfloat16 [2, 256, 512, 128], P(None, 'mom', 'pts'), may hold values from -0.25 to 0.25
- screened: bfloat16 [2, 256, 512, 512], P(None, None, ('pts', 'mom')), may hold values from -12 to 12
- val_energy: float32 [256, 64], P('mom', 'pts'), may hold values from -2 to -0.5
- cond_energy: float32 [256, 128], P('mom'), may hold values from 0.5 to 2
- grid_of_slot: int32 [256], replicated, may hold values from 0 to 255, as said below
- opposite_slot: int32 [256], P('mom'), may hold values from 0 to 255, as said below
Outputs:
- applied: float32 [2, 2, 1, 256, 64, 128], P(None, None, None, 'mom', 'pts')
Inputs may be any that keep to these rules, and one draw needn't show every extreme that they name: `grid_of_slot`: a permutation of the grid indices. opposite_slot[s] is the slot whose grid index is 255 - grid_of_slot[s]; it is never s, and s and opposite_slot[s] lie in aligned blocks of 128 slots whose first slots differ by 128.
All inputs are finite; a program needn't handle non-finite values.
Results may differ from a plain program's by a relative error of at most 0.006.
Values may be sent and summed in bfloat16 or wider, within the bound.
No kernel may reach another device: no remote copies, remote signals or barrier semaphores. Data moves between devices by JAX's collectives and lax.ppermute only.
A program may use at most 256 MiB of HBM per device.

v0:
```python
import math

import jax
import jax.numpy as jnp
from jax import lax
from jax.sharding import PartitionSpec as P


def partner_2(value, axis, apart):
    mask = 2**apart
    pairs = [(source, source ^ mask) for source in range(lax.axis_size(axis))]
    return lax.ppermute(value, axis, pairs)


def complex_mix(formula, left, right, left_sign, right_sign):
    real_real = jnp.einsum(formula, left[0], right[0], preferred_element_type=jnp.float32)
    imag_imag = jnp.einsum(formula, left[1], right[1], preferred_element_type=jnp.float32)
    real_imag = jnp.einsum(formula, left[0], right[1], preferred_element_type=jnp.float32)
    imag_real = jnp.einsum(formula, left[1], right[0], preferred_element_type=jnp.float32)
    return jnp.stack(
        [
            real_real - left_sign * right_sign * imag_imag,
            right_sign * real_imag + left_sign * imag_real,
        ]
    )


def on_device(
    amplitudes,
    val_orbitals,
    cond_orbitals,
    screened,
    val_energy,
    cond_energy,
    grid_of_slot,
    opposite_slot,
):
    slots_here = opposite_slot.shape[0]
    total_slots = grid_of_slot.shape[0]
    rows_here = val_energy.shape[1]
    frequency = jnp.arange(total_slots, dtype=jnp.int32)
    phases = frequency[:, None] * grid_of_slot[None, :] % total_slots
    angles = phases.astype(jnp.float32) * (2.0 * math.pi / total_slots)
    cosine_table = jnp.cos(angles).astype(jnp.bfloat16)
    sine_table = jnp.sin(angles).astype(jnp.bfloat16)
    half_product = complex_mix("bnkvc,kuc->bnkvu", amplitudes, cond_orbitals, 1.0, 1.0).astype(
        jnp.bfloat16
    )
    pair_values = complex_mix("bnkvu,kvm->bnkum", half_product, val_orbitals, 1.0, -1.0).astype(
        jnp.bfloat16
    )
    flattened = pair_values.reshape(pair_values.shape[:4] + (-1,))
    weights = screened.reshape(2, total_slots, -1)
    inverse_count = 1.0 / total_slots
    whole_k = lax.all_to_all(flattened, "mom", split_axis=4, concat_axis=3, tiled=True)
    spec_real = jnp.einsum(
        "fs,bnsc->bnfc", cosine_table, whole_k[0], preferred_element_type=jnp.float32
    ) + jnp.einsum("fs,bnsc->bnfc", sine_table, whole_k[1], preferred_element_type=jnp.float32)
    spec_imag = jnp.einsum(
        "fs,bnsc->bnfc", cosine_table, whole_k[1], preferred_element_type=jnp.float32
    ) - jnp.einsum("fs,bnsc->bnfc", sine_table, whole_k[0], preferred_element_type=jnp.float32)
    prod_real = (weights[0] * spec_real - weights[1] * spec_imag).astype(jnp.bfloat16)
    prod_imag = (weights[0] * spec_imag + weights[1] * spec_real).astype(jnp.bfloat16)
    back_real = (
        jnp.einsum("fs,bnfc->bnsc", cosine_table, prod_real, preferred_element_type=jnp.float32)
        - jnp.einsum("fs,bnfc->bnsc", sine_table, prod_imag, preferred_element_type=jnp.float32)
    ) * inverse_count
    back_imag = (
        jnp.einsum("fs,bnfc->bnsc", cosine_table, prod_imag, preferred_element_type=jnp.float32)
        + jnp.einsum("fs,bnfc->bnsc", sine_table, prod_real, preferred_element_type=jnp.float32)
    ) * inverse_count
    field_pts = lax.all_to_all(
        jnp.stack([back_real, back_imag]).astype(jnp.bfloat16),
        "mom",
        split_axis=3,
        concat_axis=4,
        tiled=True,
    )
    field_pts = field_pts.reshape(pair_values.shape)
    weighted = complex_mix("bnkum,kvm->bnkvu", field_pts, val_orbitals, 1.0, 1.0).astype(
        jnp.bfloat16
    )
    rows_mine = lax.all_to_all(weighted, "pts", split_axis=4, concat_axis=5, tiled=True)
    band_values = complex_mix(
        "bnkvu,kuc->bnkvc",
        rows_mine,
        lax.all_gather(cond_orbitals, "pts", axis=2, tiled=True),
        1.0,
        -1.0,
    )
    top_bit = lax.axis_size("mom").bit_length() - 2
    partner = partner_2(band_values.astype(jnp.bfloat16), "mom", top_bit).astype(band_values.dtype)
    mirrored = jnp.take(partner, opposite_slot % slots_here, axis=3)
    start_row = lax.axis_index("pts") * rows_here
    own_rows = lax.dynamic_slice_in_dim(amplitudes, start_row, rows_here, 4).astype(jnp.float32)
    energy_gap = cond_energy[:, None, :] - val_energy[:, :, None]
    result_real = energy_gap * own_rows[0, 0] - band_values[0, 0] - mirrored[0, 1]
    result_imag = energy_gap * own_rows[1, 0] - band_values[1, 0] + mirrored[1, 1]
    anti_real = -energy_gap * own_rows[0, 1] + band_values[0, 1] + mirrored[0, 0]
    anti_imag = -energy_gap * own_rows[1, 1] + band_values[1, 1] - mirrored[1, 0]
    return jnp.stack([jnp.stack([result_real, anti_real]), jnp.stack([result_imag, anti_imag])])


def solution(mesh):
    in_specs = (
        P(None, None, None, "mom", None, None),
        P(None, "mom", None, None),
        P(None, "mom", "pts", None),
        P(None, None, ("pts", "mom"), None),
        P("mom", "pts"),
        P("mom", None),
        P(),
        P("mom"),
    )
    out_specs = P(None, None, None, "mom", "pts", None)
    return jax.shard_map(
        on_device, mesh=mesh, in_specs=in_specs, out_specs=out_specs, check_vma=False
    )
```

profile of v0, /device:TPU:0, one launch (start us, length us, event | category | flops | bytes accessed | tf_op | source)
XLA Modules:
  0.0 1007.6 jit_solution(14866260467784046337)
XLA Ops:
  6.5 0.7 all-gather.2.cloned.1.call-update
  7.3 4.6 fusion.134
  11.9 4.1 fusion.41
  16.0 4.1 fusion.40
  20.1 5.4 fusion.44
  25.5 5.4 fusion.45
  30.9 9.8 fusion.17
  40.7 14.0 %fusion.34 = bf16[2,1,128,32,512]{4,3,0,2,1:T(8,128)(2,1)} fusion(f32[128,2,32,512]{3,2,1,0:T(8,128)} %fusion.17, bf16[2,128,64,32]{2,3,0,1:T(8,128)(2,1)} %fusion.45, bf16[2,128,64,512]{3,2,1,0:T(8,128)(2,1)} %param.9), kind=kOutput, calls=%fused_computation.51 | convolution fusion | flops 549453824 | bytes 35651584 | tf_op jit(solution)/shard_map/bnkvu,kvm->bnkum/dot_general | solution.py:17
  54.7 16.5 %copy.203 = bf16[2,1,128,32,512]{2,0,4,3,1:T(2,128)(2,1)} copy(bf16[2,1,128,32,512]{4,3,0,2,1:T(8,128)(2,1)} %fusion.34) | data formatting | bytes 16777216 | tf_op jit(solution)/shard_map/stack | solution.py:20
  71.2 12.1 %fusion.23 = f32[128,2,32,512]{3,2,1,0:T(8,128)} fusion(bf16[2,128,64,32]{2,3,0,1:T(8,128)(2,1)S(1)} %copy-done.4, bf16[2,128,64,512]{3,2,1,0:T(8,128)(2,1)} %param.9), kind=kOutput, calls=%fused_computation.40 | convolution fusion | flops 536870912 | bytes 26214400 | tf_op jit(solution)/shard_map/bnkvu,kvm->bnkum/dot_general | solution.py:18
  83.4 12.9 %fusion.37 = bf16[2,1,128,32,512]{4,3,0,2,1:T(8,128)(2,1)} fusion(bf16[2,128,64,32]{2,3,0,1:T(8,128)(2,1)S(1)} %copy-done.2, bf16[2,128,64,512]{3,2,1,0:T(8,128)(2,1)} %param.9, f32[128,2,32,512]{3,2,1,0:T(8,128)} %fusion.23), kind=kOutput, calls=%fused_computation.52 | convolution fusion | flops 549453824 | bytes 34603008 | tf_op jit(solution)/shard_map/bnkvu,kvm->bnkum/dot_general | solution.py:19
  96.3 15.7 %copy.204 = bf16[2,1,128,32,512]{2,0,4,3,1:T(2,128)(2,1)} copy(bf16[2,1,128,32,512]{4,3,0,2,1:T(8,128)(2,1)} %fusion.37) | data formatting | bytes 16777216 | tf_op jit(solution)/shard_map/stack | solution.py:20
  112.0 26.4 %pad_maximum_fusion = bf16[2,2,1,128,16384]{3,1,2,0,4:T(2,128)(2,1)} fusion(bf16[1,2,1,128,16384]{3,1,2,0,4:T(2,128)(2,1)} %bitcast.316, bf16[1,2,1,128,16384]{3,1,2,0,4:T(2,128)(2,1)} %bitcast.315), kind=kLoop, calls=%fused_computation.3 | loop fusion | flops 8388608 | bytes 33554432 | tf_op jit(solution)/shard_map/stack | solution.py:20
  138.4 9.8 all-to-all-start
  148.2 12.1 %slice_convert_fusion.1 = (f32[1,256,16,512]{3,2,1,0:T(8,128)}, f32[1,256,16,512]{3,2,1,0:T(8,128)}) fusion(bf16[2,256,16,512]{3,2,1,0:T(8,128)(2,1)} %param.11), kind=kLoop, calls=%fused_computation.61 | loop fusion | flops 4194304 | bytes 25165824 | tf_op jit(solution)/shard_map/convert_element_type | solution.py:62
  160.3 9.9 copy.202
  170.2 10.0 copy.205
  180.2 150.9 %all-to-all-done = bf16[2,2,1,128,16384]{3,1,2,0,4:T(2,128)(2,1)} async-done(((bf16[2,2,1,128,16384]{3,1,2,0,4:T(2,128)(2,1)}), bf16[2,2,1,128,16384]{3,1,2,0,4:T(2,128)(2,1)}, u32[]{:S(2)}, u32[]{:S(2)}) %all-to-all-start) | async-done | bytes 16777248 | tf_op jit(solution)/shard_map/all_to_all | solution.py:55
  331.1 28.1 %copy.246 = bf16[2,2,1,128,2,8192]{3,4,5,1,2,0:T(2,128)(2,1)S(1)} copy(bf16[2,2,1,128,2,8192]{3,1,0,5,4,2:T(2,128)(2,1)} %bitcast.38) | data formatting | bytes 33554432 | tf_op jit(solution)/shard_map/all_to_all | solution.py:55
  359.2 13.0 %fusion.133 = (bf16[1,2,1,2,128,8192]{4,3,5,1,2,0:T(2,128)(2,1)}, bf16[1,2,1,2,128,8192]{4,3,5,1,2,0:T(2,128)(2,1)}) fusion(bf16[2,2,1,2,128,8192]{4,3,5,1,2,0:T(2,128)(2,1)S(1)} %bitcast.312), kind=kLoop, calls=%fused_computation.179 | loop fusion | bytes 33554432 | tf_op jit(solution)/shard_map/slice | solution.py:58
  372.2 14.1 %reshape.539 = bf16[2,256,8192]{1,2,0:T(8,128)(2,1)} reshape(bf16[1,2,1,2,128,8192]{4,3,5,1,2,0:T(2,128)(2,1)} %get-tuple-element.15) | data formatting | bytes 16777216 | tf_op jit(solution)/shard_map/reshape.28
  386.3 14.2 %reshape.538 = bf16[2,256,8192]{1,2,0:T(8,128)(2,1)} reshape(bf16[1,2,1,2,128,8192]{4,3,5,1,2,0:T(2,128)(2,1)} %get-tuple-element.16) | data formatting | bytes 16777216 | tf_op jit(solution)/shard_map/reshape.24
  400.5 12.5 %fusion.91 = f32[2,8192,256]{2,1,0:T(8,128)} fusion(bf16[2,256,8192]{1,2,0:T(8,128)(2,1)} %reshape.539, s32[256]{0:T(256)S(1)} %copy-done.6), kind=kOutput, calls=%fused_computation.134 | convolution fusion | flops 2148466688 | bytes 25166848 | tf_op jit(solution)/shard_map/fs,bnsc->bnfc/dot_general | solution.py:59
  413.1 9.0 fusion.93
  422.1 14.8 %convolution_subtract_fusion = f32[2,8192,256]{2,1,0:T(8,128)} fusion(f32[2,8192,256]{2,1,0:T(8,128)} %fusion.91, bf16[2,256,8192]{1,2,0:T(8,128)(2,1)S(1)} %copy-done.1, s32[256]{0:T(256)S(1)} %copy-done.6), kind=kOutput, calls=%fused_computation.23 | convolution fusion | flops 2152660992 | bytes 41944064 | tf_op jit(solution)/shard_map/fs,bnsc->bnfc/dot_general | solution.py:61
  436.9 27.2 %fusion.11 = (bf16[2,256,8192]{1,2,0:T(8,128)(2,1)}, bf16[2,256,8192]{1,2,0:T(8,128)(2,1)}) fusion(f32[2,8192,256]{2,1,0:T(8,128)} %convolution_subtract_fusion, f32[256,8192]{0,1:T(8,128)} %bitcast.311, f32[256,8192]{0,1:T(8,128)} %bitcast.310, f32[2,8192,256]{2,1,0:T(8,128)} %fusion.93, bf16[2,256,8192]{1,2,0:T(8,128)(2,1)} %reshape.539, s32[256]{0:T(256)S(1)} %copy-done.6), kind=kOutput, calls=%fused_computation.28 | convolution fusion | flops 2186215424 | bytes 75498496 | tf_op jit(solution)/shard_map/fs,bnsc->bnfc/dot_general | solution.py:58
  464.1 12.5 %fusion.89 = f32[2,8192,256]{2,1,0:T(8,128)} fusion(bf16[2,256,8192]{1,2,0:T(8,128)(2,1)} %get-tuple-element.11, s32[256]{0:T(256)S(1)} %copy-done.6), kind=kOutput, calls=%fused_computation.133 | convolution fusion | flops 2148466688 | bytes 25166848 | tf_op jit(solution)/shard_map/fs,bnfc->bnsc/dot_general | solution.py:65
  476.7 9.0 fusion.87
  485.7 13.5 %fusion.8 = bf16[1,2,1,256,8192]{3,4,1,2,0:T(8,128)(2,1)} fusion(f32[2,8192,256]{2,1,0:T(8,128)} %fusion.89, bf16[2,256,8192]{1,2,0:T(8,128)(2,1)} %get-tuple-element.12, s32[256]{0:T(256)S(1)} %copy-done.6), kind=kOutput, calls=%fused_computation.25 | convolution fusion | flops 2161049600 | bytes 33555456 | tf_op jit(solution)/shard_map/fs,bnfc->bnsc/dot_general | solution.py:66
  499.2 11.5 %fusion.9 = bf16[1,2,1,256,8192]{3,4,1,2,0:T(8,128)(2,1)} fusion(f32[2,8192,256]{2,1,0:T(8,128)} %fusion.87, bf16[2,256,8192]{1,2,0:T(8,128)(2,1)S(1)} %bitcast.309, s32[256]{0:T(256)S(1)} %copy-done.6), kind=kOutput, calls=%fused_computation.26 | convolution fusion | flops 2161049600 | bytes 33555456 | tf_op jit(solution)/shard_map/fs,bnfc->bnsc/dot_general | solution.py:70
  510.8 13.7 %pad_maximum_fusion.1 = bf16[2,2,1,256,8192]{3,4,1,2,0:T(8,128)(2,1)} fusion(bf16[1,2,1,256,8192]{3,4,1,2,0:T(8,128)(2,1)} %fusion.9, bf16[1,2,1,256,8192]{3,4,1,2,0:T(8,128)(2,1)} %fusion.8), kind=kLoop, calls=%fused_computation.4 | loop fusion | flops 8388608 | bytes 33554432 | tf_op jit(solution)/shard_map/stack | solution.py:73
  524.5 41.2 %copy.175 = bf16[2,2,1,256,8192]{4,1,2,0,3:T(2,128)(2,1)} copy(bf16[2,2,1,256,8192]{3,4,1,2,0:T(8,128)(2,1)} %pad_maximum_fusion.1) | data formatting | bytes 33554432 | tf_op jit(solution)/shard_map/stack | solution.py:73
  565.7 200.1 %all_to_all.45 = bf16[2,2,1,256,8192]{4,1,2,0,3:T(2,128)(2,1)} all-to-all(bf16[2,2,1,256,8192]{4,1,2,0,3:T(2,128)(2,1)} %copy.175), channel_id=1, replica_groups=mesh['mom'=2,'pts'=16] {'mom'}, dimensions={3} | all-to-all | bytes 33554432 | tf_op jit(solution)/shard_map/all_to_all | solution.py:72
  765.8 30.2 %copy.245 = bf16[2,2,1,2,128,8192]{5,3,1,4,2,0:T(2,128)(2,1)S(1)} copy(bf16[2,2,1,2,128,8192]{5,1,0,4,3,2:T(2,128)(2,1)} %bitcast.314) | data formatting | bytes 33554432 | tf_op jit(solution)/shard_map/all_to_all | solution.py:72
  796.1 14.9 %fusion.132 = (bf16[1,2,1,128,2,8192]{5,4,1,3,2,0:T(2,128)(2,1)}, bf16[1,2,1,128,2,8192]{5,4,1,3,2,0:T(2,128)(2,1)}) fusion(bf16[2,2,1,128,2,8192]{5,4,1,3,2,0:T(2,128)(2,1)S(1)} %bitcast.313), kind=kLoop, calls=%fused_computation.178 | loop fusion | bytes 33554432 | tf_op jit(solution)/shard_map/slice | solution.py:16
  811.0 14.3 %reshape.542 = bf16[2,128,32,512]{3,2,0,1:T(8,128)(2,1)} reshape(bf16[1,2,1,128,2,8192]{5,4,1,3,2,0:T(2,128)(2,1)} %get-tuple-element.13) | data formatting | bytes 16777216 | tf_op jit(solution)/shard_map/reshape.50
  825.2 14.3 %reshape.543 = bf16[2,128,32,512]{3,2,0,1:T(8,128)(2,1)} reshape(bf16[1,2,1,128,2,8192]{5,4,1,3,2,0:T(2,128)(2,1)} %get-tuple-element.14) | data formatting | bytes 16777216 | tf_op jit(solution)/shard_map/reshape.54
  839.5 10.1 fusion.14
  849.6 10.1 fusion.12
  859.6 9.3 fusion.46
  868.9 10.7 %fusion.47 = bf16[1,2,1,128,64,32]{4,5,1,3,2,0:T(8,128)(2,1)} fusion(f32[128,2,32,64]{3,2,1,0:T(8,128)} %fusion.12, bf16[2,128,32,512]{3,2,0,1:T(8,128)(2,1)} %reshape.542, bf16[2,128,64,512]{3,2,1,0:T(8,128)(2,1)} %param.9), kind=kOutput, calls=%fused_computation.69 | convolution fusion | flops 537919488 | bytes 22020096 | tf_op jit(solution)/shard_map/bnkum,kvm->bnkvu/dot_general | solution.py:18
  879.6 4.6 pad_maximum_fusion.2
  884.2 8.0 copy.177
  892.1 52.0 %all_to_all.46 = bf16[2,2,1,128,64,32]{3,5,2,1,0,4:T(8,128)(2,1)S(1)} all-to-all(bf16[2,2,1,128,64,32]{3,5,2,1,0,4:T(8,128)(2,1)S(1)} %copy.177), channel_id=1, replica_groups=mesh['mom'=2,'pts'=16] {'pts'}, dimensions={4} | all-to-all | bytes 4194304 | tf_op jit(solution)/shard_map/all_to_all | solution.py:83
  944.1 0.4 copy.178
  944.5 1.4 fusion.135
  946.0 0.9 copy.182
  946.9 1.3 copy.179
  948.3 0.9 copy.180
  949.2 7.0 fusion.5
  956.3 7.1 fusion.6
  963.3 7.0 fusion.4
  970.4 7.1 fusion.7
  977.5 1.4 fusion.128
  978.9 0.4 collective-permute-start
  979.3 1.5 constant_dynamic-slice_fusion
  980.8 0.1 copy_convert_fusion
  980.9 12.8 %collective-permute-done = bf16[2,2,1,128,4,128]{5,3,4,2,1,0:T(8,128)(2,1)S(1)} collective-permute-done((bf16[2,2,1,128,4,128]{5,3,4,2,1,0:T(8,128)(2,1)S(1)}, bf16[2,2,1,128,4,128]{5,3,4,2,1,0:T(8,128)(2,1)S(1)}, u32[]{:S(2)}, u32[]{:S(2)}) %collective-permute-start) | collective-permute-done | bytes 524320 | tf_op jit(solution)/shard_map/ppermute | solution.py:12
  993.9 0.7 copy.190
  994.6 1.4 gather_fusion
  995.9 0.4 bitcast_select_fusion
  996.3 1.1 fusion.65
  997.4 1.3 fusion.73
  999.0 1.6 copy.195
  (42 shorter events, 0.5 us)
Async XLA Ops:
  6.5 942.7 %all-gather.2.cloned.1.call-start = ((), (), s32[]{:S(2)}) async-start(), calls=%async_computation.3 | async-start | bytes 35651584 | tf_op jit(solution)/shard_map/all_gather | solution.py:87
  7.3 4.6 copy-start.3
  16.0 14.9 %slice-start = ((s8[16777216]{0:T(1024)(128)(4,1)}), s8[4194304]{0:T(1024)(128)(4,1)S(1)}, s32[]{:S(2)}) async-start(s8[16777216]{0:T(1024)(128)(4,1)} %bitcast.306), calls=%async_computation.4 | async-start | bytes 8388608
  16.0 14.9 %slice-start.1 = ((s8[16777216]{0:T(1024)(128)(4,1)}), s8[4194304]{0:T(1024)(128)(4,1)S(1)}, s32[]{:S(2)}) async-start(s8[16777216]{0:T(1024)(128)(4,1)} %bitcast.306), calls=%async_computation.5 | async-start | bytes 8388608
  20.0 10.8 %slice-start.2 = ((s8[16777216]{0:T(1024)(128)(4,1)}), s8[4194304]{0:T(1024)(128)(4,1)S(1)}, s32[]{:S(2)}) async-start(s8[16777216]{0:T(1024)(128)(4,1)} %bitcast.306), calls=%async_computation.6 | async-start | bytes 8388608
  25.5 5.4 slice-start.3
  54.7 16.5 %copy-start.4 = (bf16[2,128,64,32]{2,3,0,1:T(8,128)(2,1)S(1)}, bf16[2,128,64,32]{2,3,0,1:T(8,128)(2,1)}, u32[]{:S(2)}) copy-start(bf16[2,128,64,32]{2,3,0,1:T(8,128)(2,1)} %fusion.44) | copy-start | bytes 3145732
  71.2 12.1 %copy-start.2 = (bf16[2,128,64,32]{2,3,0,1:T(8,128)(2,1)S(1)}, bf16[2,128,64,32]{2,3,0,1:T(8,128)(2,1)}, u32[]{:S(2)}) copy-start(bf16[2,128,64,32]{2,3,0,1:T(8,128)(2,1)} %fusion.45) | copy-start | bytes 3145732
  138.4 192.7 %all-to-all-start = ((bf16[2,2,1,128,16384]{3,1,2,0,4:T(2,128)(2,1)}), bf16[2,2,1,128,16384]{3,1,2,0,4:T(2,128)(2,1)}, u32[]{:S(2)}, u32[]{:S(2)}) async-start(bf16[2,2,1,128,16384]{3,1,2,0,4:T(2,128)(2,1)} %pad_maximum_fusion), calls=%async_computation | async-start | bytes 33554432 | tf_op jit(solution)/shard_map/all_to_all | solution.py:55
  386.3 14.2 %copy-start.6 = (s32[256]{0:T(256)S(1)}, s32[256]{0:T(256)}, u32[]{:S(2)}) copy-start(s32[256]{0:T(256)} %param.14) | copy-start | bytes 3076
  400.5 12.6 %copy-start.1 = (bf16[2,256,8192]{1,2,0:T(8,128)(2,1)S(1)}, bf16[2,256,8192]{1,2,0:T(8,128)(2,1)}, u32[]{:S(2)}) copy-start(bf16[2,256,8192]{1,2,0:T(8,128)(2,1)} %reshape.538) | copy-start | bytes 25165828
  464.1 12.6 %copy-start = (bf16[2,256,8192]{1,2,0:T(8,128)(2,1)S(1)}, bf16[2,256,8192]{1,2,0:T(8,128)(2,1)}, u32[]{:S(2)}) copy-start(bf16[2,256,8192]{1,2,0:T(8,128)(2,1)} %get-tuple-element.12) | copy-start | bytes 25165828
  464.1 35.1 %slice-start.4 = ((s8[8388608]{0:T(1024)(128)(4,1)}), s8[4194304]{0:T(1024)(128)(4,1)S(1)}, s32[]{:S(2)}) async-start(s8[8388608]{0:T(1024)(128)(4,1)} %bitcast.308), calls=%async_computation.8 | async-start | bytes 8388608
  476.7 22.5 %slice-start.5 = ((s8[8388608]{0:T(1024)(128)(4,1)}), s8[4194304]{0:T(1024)(128)(4,1)S(1)}, s32[]{:S(2)}) async-start(s8[8388608]{0:T(1024)(128)(4,1)} %bitcast.308), calls=%async_computation.9 | async-start | bytes 8388608
  970.4 8.9 copy-start.8
  977.5 18.9 %copy-start.5 = (f32[128,128]{1,0:T(8,128)S(1)}, f32[128,128]{1,0:T(8,128)}, u32[]{:S(2)}) copy-start(f32[128,128]{1,0:T(8,128)} %param.13) | copy-start | bytes 196612
  977.5 18.9 %copy-start.7 = (f32[128,4]{0,1:T(4,128)S(1)}, f32[128,4]{0,1:T(4,128)}, u32[]{:S(2)}) copy-start(f32[128,4]{0,1:T(4,128)} %param.12) | copy-start | bytes 6148
  978.9 14.9 %collective-permute-start = (bf16[2,2,1,128,4,128]{5,3,4,2,1,0:T(8,128)(2,1)S(1)}, bf16[2,2,1,128,4,128]{5,3,4,2,1,0:T(8,128)(2,1)S(1)}, u32[]{:S(2)}, u32[]{:S(2)}) collective-permute-start(bf16[2,2,1,128,4,128]{5,3,4,2,1,0:T(8,128)(2,1)S(1)} %pad_maximum_fusion.4), channel_id=1, source_target_pairs={{0,16},{16,0},{1,17},{17,1},{2,18},{18,2},{3,19},{19,3},{4,20},{20... | collective-permute-start | bytes 1572872 | tf_op jit(solution)/shard_map/ppermute | solution.py:12
Sparse Core Ops, SparseCore 0:
  8.9 170.7 all-gather.1
where the time goes:
time: 1020 us; the launch traced here: 1010 us
  local copies, waits for them, and re-layouts  259 us (25%)
  blocking collectives  252 us (25%)
  matrix products  246 us (24%)
  waiting for transfers between devices  164 us (16%)
  other arithmetic  61.5 us (6%)
  between operations  13.9 us (1%)
    all_to_all x1, blocking collectives, on_device(): lax.all_to_all(jnp.stack([back_real, back_imag]).astype(jnp.bfloat16), 'm...  200 us
    all_to_all x1, waiting for transfers between devices, on_device(): lax.all_to_all(flattened, 'mom', split_axis=4, concat_axis=3, tiled=True)  151 us
    another operation x6, local copies, waits for them, and re-layouts  58.6 us
    all_to_all x1, blocking collectives, on_device(): lax.all_to_all(weighted, 'pts', split_axis=4, concat_axis=5, tiled=True)  52 us
    another operation x1, local copies, waits for them, and re-layouts, on_device(): jnp.stack([back_real, back_imag]).astype(jnp.bfloat16)  41.2 us
    another operation x3, local copies, waits for them, and re-layouts, complex_mix(): jnp.stack([real_real - left_sign * right_sign * imag_imag, right_sign * r...  40.2 us
    dot_general x4, matrix products, complex_mix(): jnp.einsum(formula, left[1], right[1], preferred_element_type=jnp.float32)  35.8 us
    dot_general x4, matrix products, complex_mix(): jnp.einsum(formula, left[1], right[0], preferred_element_type=jnp.float32)  35.4 us
  transfers between devices with their start and end apart: 3, of which 2 were waited for; matrix products, arithmetic and copies ran while one was open for 53% of the time, Pallas kernels for 0%

commit v1 on v0

--- a/solution.py
+++ b/solution.py
@@ -1,9 +1,16 @@
+import functools
 import math
 
 import jax
 import jax.numpy as jnp
 from jax import lax
+from jax.experimental import pallas as pl
+from jax.experimental.pallas import tpu as pltpu
 from jax.sharding import PartitionSpec as P
+
+F32 = jnp.float32
+BF16 = jnp.bfloat16
+MIB = 1024 * 1024
 
 
 def partner_2(value, axis, apart):
@@ -25,7 +32,7 @@
     )
 
 
-def on_device(
+def general_path(
     amplitudes,
     val_orbitals,
     cond_orbitals,
@@ -101,6 +108,407 @@
     return jnp.stack([jnp.stack([result_real, anti_real]), jnp.stack([result_imag, anti_imag])])
 
 
+def half_signs(low, high):
+    lane = lax.broadcasted_iota(jnp.int32, (1, 128), 1)
+    return jnp.where(lane < 64, low, high).astype(F32)
+
+
+def half_body(where_ref, amp_ref, cond_ref, out_ref):
+    groups, block, _, points, _ = out_ref.shape
+    total = groups * points
+    signs = half_signs(-1.0, 1.0)
+    for kk in range(block):
+        cond = cond_ref[:, kk].reshape(2 * total, cond_ref.shape[-1])
+        for b in range(2):
+            amp = amp_ref[:, b, 0, kk].reshape(128, amp_ref.shape[-1])
+            full = lax.dot_general(
+                cond, amp, (((1,), (1,)), ((), ())), preferred_element_type=F32
+            )
+            half = full[:total] + pltpu.roll(full[total:], 64, 1) * signs
+            half = half.astype(BF16).reshape(groups, points, 128)
+            for g in range(groups):
+                out_ref[where_ref[g], kk, b] = half[g]
+
+
+def half_call(amplitudes, cond_orbitals, where, groups):
+    slots, bands = amplitudes.shape[3], amplitudes.shape[5]
+    rows = amplitudes.shape[4]
+    points = cond_orbitals.shape[2] // groups
+    block = 16
+    return pl.pallas_call(
+        half_body,
+        out_shape=jax.ShapeDtypeStruct((groups, slots, 2, points, 128), BF16),
+        grid_spec=pltpu.PrefetchScalarGridSpec(
+            num_scalar_prefetch=1,
+            grid=(slots // block,),
+            in_specs=[
+                pl.BlockSpec((2, 2, 1, block, rows, bands), lambda i, *_: (0, 0, 0, i, 0, 0)),
+                pl.BlockSpec((2, block, groups * points, bands), lambda i, *_: (0, i, 0, 0)),
+            ],
+            out_specs=pl.BlockSpec(
+                (groups, block, 2, points, 128), lambda i, *_: (0, i, 0, 0, 0)
+            ),
+        ),
+        compiler_params=pltpu.CompilerParams(vmem_limit_bytes=40 * MIB),
+    )(where, amplitudes, cond_orbitals)
+
+
+def main_body(layout, base_ref, pos_ref, *refs):
+    own_blocks, block, sizes, points, first, last = layout
+    half_own, half_other, own_ref = refs[:3]
+    count = sum(len(group) for group in sizes)
+    flat = list(refs[3 : 3 + count])
+    groups = []
+    for group in sizes:
+        groups.append([flat.pop(0) for _ in group])
+    rest = list(refs[3 + count :])
+    screen_ref, forward_ref, backward_ref = rest[:3]
+    rest = rest[3:]
+    before_ref = None if first else rest.pop(0)
+    out_ref, pair_ref = rest
+    blocks = own_blocks + len(groups)
+    total = blocks * block
+    rows = 4 * points
+    lanes = pair_ref.shape[0]
+    width = lanes * 128
+    step = pl.program_id(0)
+    into = half_signs(1.0, -1.0)
+    back = half_signs(-1.0, 1.0)
+
+    def make_pairs(source, half_ref, half_start, start, size):
+        for kk in range(size):
+            half = half_ref[half_start + kk].reshape(2 * points, 128)
+            turned = (pltpu.roll(half.astype(F32), 64, 1) * into).astype(BF16)
+            stacked = jnp.concatenate([half, turned], axis=0)
+            val = source[:, kk].reshape(128, width)
+            pairs = jnp.dot(stacked, val, preferred_element_type=F32)
+            at = pl.multiple_of((start + kk) * rows, rows)
+            for l in range(lanes):
+                pair_ref[l, pl.ds(at, rows), :] = pairs[:, l * 128 : (l + 1) * 128]
+
+    def make_weighted(source, half_ref, half_start, start, size):
+        for kk in range(size):
+            k = start + kk
+            at = pl.multiple_of(k * rows, rows)
+            field = jnp.concatenate(
+                [pair_ref[l, pl.ds(at, rows), :] for l in range(lanes)], axis=1
+            ).astype(BF16)
+            val = source[:, kk].reshape(128, width)
+            both = lax.dot_general(
+                field, val, (((1,), (1,)), ((), ())), preferred_element_type=F32
+            )
+            half = rows // 2
+            weighted = both[:half] + pltpu.roll(both[half:], 64, 1) * back
+            if not first:
+                weighted = before_ref[k] + weighted
+            if last:
+                out_ref[pos_ref[k]] = weighted.astype(BF16).reshape(2, points, 128)
+            else:
+                out_ref[k] = weighted
+
+    def each_block(work, index):
+        @pl.when(index < own_blocks)
+        def _():
+            work(own_ref, half_own, index * block, index * block, block)
+
+        for t, (group, extents) in enumerate(zip(groups, sizes)):
+
+            @pl.when(index == own_blocks + t)
+            def _():
+                done = 0
+                for ref, extent in zip(group, extents):
+                    start = (own_blocks + t) * block + done
+                    work(ref, half_other, base_ref[t] + done, start, extent)
+                    done += extent
+
+    @pl.when(step < blocks)
+    def _():
+        each_block(make_pairs, step)
+
+    @pl.when((step >= blocks) & (step < blocks + points))
+    def _():
+        nu = step - blocks
+        for l in range(lanes):
+            columns = []
+            for b in range(2):
+                parts = []
+                for ri in range(2):
+                    row = ri * 2 * points + b * points + nu
+                    parts.append(pair_ref[l, pl.ds(row, total, stride=rows), :].astype(BF16))
+                columns.append(jnp.concatenate(parts, axis=0))
+            spectrum = jnp.dot(
+                forward_ref[...], jnp.concatenate(columns, axis=1), preferred_element_type=F32
+            )
+            real = screen_ref[0, 0, :, l * 128 : (l + 1) * 128].astype(F32)
+            imag = screen_ref[0, 1, :, l * 128 : (l + 1) * 128].astype(F32)
+            real = jnp.concatenate([real, real], axis=1)
+            imag = jnp.concatenate([imag, imag], axis=1)
+            spec_real, spec_imag = spectrum[:total], spectrum[total:]
+            prod_real = (real * spec_real - imag * spec_imag).astype(BF16)
+            prod_imag = (real * spec_imag + imag * spec_real).astype(BF16)
+            field = jnp.dot(
+                backward_ref[...],
+                jnp.concatenate([prod_real, prod_imag], axis=0),
+                preferred_element_type=F32,
+            )
+            for b in range(2):
+                for ri in range(2):
+                    row = ri * 2 * points + b * points + nu
+                    pair_ref[l, pl.ds(row, total, stride=rows), :] = field[
+                        ri * total : (ri + 1) * total, b * 128 : (b + 1) * 128
+                    ]
+
+    @pl.when(step >= blocks + points)
+    def _():
+        each_block(make_weighted, step - blocks - points)
+
+
+def main_call(half_own, half_other, own, chunk, pieces, screen, tables, base, pos, before, last):
+    slots, _, points, _ = half_own.shape
+    bands = own.shape[2]
+    block = sum(piece.shape[1] for piece in pieces[0])
+    width = pieces[0][0].shape[3]
+    own_blocks = slots // block
+    blocks = own_blocks + len(pieces)
+    total = blocks * block
+    first = before is None
+    sizes = tuple(tuple(piece.shape[1] for piece in group) for group in pieces)
+    flat = [piece for group in pieces for piece in group]
+
+    def own_map(s, *_):
+        early = jnp.minimum(s, own_blocks - 1)
+        late = jnp.clip(s - blocks - points, 0, own_blocks - 1)
+        return (0, jnp.where(s < blocks, early, late), 0, chunk)
+
+    def whole(shape):
+        return pl.BlockSpec(
+            shape, lambda s, *_: (0,) * len(shape), pipeline_mode=pl.Buffered(1)
+        )
+
+    in_specs = [
+        whole(half_own.shape),
+        whole(half_other.shape),
+        pl.BlockSpec((2, block, bands, width), own_map),
+    ]
+    in_specs += [whole(piece.shape) for piece in flat]
+    in_specs += [
+        pl.BlockSpec(
+            (1, 2, total, width), lambda s, *_: (jnp.clip(s - blocks, 0, points - 1), 0, 0, chunk)
+        ),
+        whole(tables[0].shape),
+        whole(tables[1].shape),
+    ]
+    operands = [half_own, half_other, own, *flat, screen, *tables]
+    if not first:
+        in_specs.append(whole(before.shape))
+        operands.append(before)
+    if last:
+        out = jax.ShapeDtypeStruct((total, 2, points, 128), BF16)
+    else:
+        out = jax.ShapeDtypeStruct((total, 2 * points, 128), F32)
+    return pl.pallas_call(
+        functools.partial(main_body, (own_blocks, block, sizes, points, first, last)),
+        out_shape=out,
+        grid_spec=pltpu.PrefetchScalarGridSpec(
+            num_scalar_prefetch=2,
+            grid=(2 * blocks + points,),
+            in_specs=in_specs,
+            out_specs=whole(out.shape),
+            scratch_shapes=[pltpu.VMEM((width // 128, total * 4 * points, 128), F32)],
+        ),
+        compiler_params=pltpu.CompilerParams(vmem_limit_bytes=60 * MIB),
+    )(base, pos, *operands)
+
+
+def final_body(weighted_ref, cond_ref, out_ref, lay_ref):
+    sources = weighted_ref.shape[0]
+    points = weighted_ref.shape[4]
+    holders = cond_ref.shape[1]
+    groups = sources // holders
+    sums = {}
+    for h in range(2):
+        columns = []
+        for ri in range(2):
+            parts = []
+            for g in range(groups):
+                part = cond_ref[h, :, 0, ri, g * points : (g + 1) * points, :]
+                parts.append(part.reshape(holders * points, 128))
+            columns.append(jnp.concatenate(parts, axis=0))
+        cond = jnp.concatenate(columns, axis=1)
+        for b in range(2):
+            weighted = weighted_ref[:, h, 0, b].reshape(sources * points, 128)
+            full = lax.dot_general(
+                weighted, cond, (((0,), (0,)), ((), ())), preferred_element_type=F32
+            )
+            sums[h, b] = (
+                full[:64, :128] + full[64:, 128:],
+                full[64:, :128] - full[:64, 128:],
+            )
+    rows = 64 // holders
+    for h in range(2):
+        here, there = sums[h, 0], sums[1 - h, 1]
+        for ri, value in enumerate((here[0] + there[0], here[1] - there[1])):
+            for p in range(holders):
+                lay_ref[p, h, ri * rows : (ri + 1) * rows, :] = value[p * rows : (p + 1) * rows]
+    out_ref[:, 0] = lay_ref[...].astype(BF16)
+
+
+def final_call(weighted, cond):
+    sources, _, pairs, _, points, _ = weighted.shape
+    holders = cond.shape[1]
+    rows = 2 * 64 // holders
+    return pl.pallas_call(
+        final_body,
+        out_shape=jax.ShapeDtypeStruct((holders, pairs, 2, rows, 128), BF16),
+        grid=(pairs,),
+        in_specs=[
+            pl.BlockSpec((sources, 2, 1, 2, points, 128), lambda i: (0, 0, i, 0, 0, 0)),
+            pl.BlockSpec(
+                (2, holders, 1, 2, cond.shape[4], 128), lambda i: (0, 0, i, 0, 0, 0)
+            ),
+        ],
+        out_specs=pl.BlockSpec((holders, 1, 2, rows, 128), lambda i: (0, i, 0, 0, 0)),
+        scratch_shapes=[pltpu.VMEM((holders, 2, rows, 128), F32)],
+        compiler_params=pltpu.CompilerParams(vmem_limit_bytes=40 * MIB),
+    )(weighted, cond)
+
+
+def swap_mom(value):
+    return lax.ppermute(value, "mom", [(0, 1), (1, 0)])
+
+
+def swap_pts(value, mask):
+    return lax.ppermute(value, "pts", [(i, i ^ mask) for i in range(lax.axis_size("pts"))])
+
+
+def other_val(part):
+    middle = part.shape[1] // 2
+    here = swap_mom(part)
+    by_y = swap_pts(here, 2)
+    by_z = swap_pts(here, 4)
+    across = [swap_pts(by_z[:, :middle], 2), swap_pts(by_y[:, middle:], 4)]
+    groups = [[here], [by_y], [by_z], across]
+    return groups + [[swap_pts(piece, 1) for piece in group] for group in groups]
+
+
+def fast_path(
+    amplitudes,
+    val_orbitals,
+    cond_orbitals,
+    screened,
+    val_energy,
+    cond_energy,
+    grid_of_slot,
+    opposite_slot,
+):
+    groups, holders = lax.axis_size("mom"), lax.axis_size("pts")
+    mom, pts = lax.axis_index("mom"), lax.axis_index("pts")
+    slots = opposite_slot.shape[0]
+    total = grid_of_slot.shape[0]
+    rows_here = val_energy.shape[1]
+    devices = groups * holders
+    pairs = slots // devices
+    points = screened.shape[2]
+    width = val_orbitals.shape[3] // CHUNKS
+    eighth = slots // 8
+
+    q = pts % 8
+    mine = lax.dynamic_slice_in_dim(val_orbitals, q * eighth, eighth, 1)
+    pieces = [other_val(mine[..., c * width : (c + 1) * width]) for c in range(CHUNKS)]
+
+    where = (jnp.arange(groups, dtype=jnp.int32) - mom) % groups
+    halves = half_call(amplitudes, cond_orbitals, where, groups)
+    half_other = swap_mom(halves[1])
+
+    order = q ^ jnp.array([0, 2, 4, 6, 1, 3, 5, 7], dtype=jnp.int32)
+    slot_own = mom * slots + jnp.arange(slots, dtype=jnp.int32)
+    slot_other = (1 - mom) * slots + (
+        order[:, None] * eighth + jnp.arange(eighth, dtype=jnp.int32)
+    ).reshape(slots)
+    slot_here = jnp.concatenate([slot_own, slot_other])
+    every = jnp.arange(total, dtype=jnp.int32)
+    is_opposite = grid_of_slot[None, :] == total - 1 - grid_of_slot[:, None]
+    opposite = jnp.sum(jnp.where(is_opposite, every[None, :], 0), axis=1)
+    low = jnp.where(every < slots, every, opposite)
+    place = low // pairs * (2 * pairs) + low % pairs + jnp.where(every < slots, 0, pairs)
+    chosen = slot_here[:, None] == every[None, :]
+    grid_here = jnp.sum(jnp.where(chosen, grid_of_slot[None, :], 0), axis=1)
+    place_here = jnp.sum(jnp.where(chosen, place[None, :], 0), axis=1)
+    phases = every[:, None] * grid_here[None, :] % total
+    angles = phases.astype(F32) * (2.0 * math.pi / total)
+    cosine = jnp.cos(angles).astype(BF16)
+    sine = jnp.sin(angles).astype(BF16)
+    forward = jnp.concatenate(
+        [jnp.concatenate([cosine, sine], 1), jnp.concatenate([-sine, cosine], 1)], 0
+    )
+    backward = forward.T * (1.0 / total)
+
+    paired = jnp.where(
+        mom == 0, jnp.arange(slots, dtype=jnp.int32), opposite[:slots] - slots
+    )
+    cond_send = jnp.take(jnp.swapaxes(cond_orbitals, 0, 1), paired, axis=0)
+    cond_send = cond_send.reshape((devices, pairs) + cond_send.shape[1:])
+    cond_pairs = lax.all_to_all(cond_send, ("mom", "pts"), 0, 0, tiled=True)
+    cond_pairs = cond_pairs.reshape((groups, holders) + cond_pairs.shape[1:])
+
+    screen = jnp.transpose(screened, (2, 0, 1, 3))
+    summed = None
+    for c in range(CHUNKS):
+        summed = main_call(
+            halves[0],
+            half_other,
+            val_orbitals,
+            c,
+            pieces[c],
+            screen,
+            (forward, backward),
+            order * eighth,
+            place_here,
+            summed,
+            c == CHUNKS - 1,
+        )
+    send = summed.reshape((devices, 2, pairs) + summed.shape[1:])
+    weighted = lax.all_to_all(send, ("mom", "pts"), 0, 0, tiled=True)
+    combined = final_call(weighted, cond_pairs)
+    combined = jnp.concatenate([combined, combined], axis=0)
+    back = lax.all_to_all(combined, ("mom", "pts"), 0, 0, tiled=True)
+
+    back = back.reshape(slots, 2, 2, rows_here, -1)
+    partner = jnp.where(
+        mom == 0, jnp.arange(slots, dtype=jnp.int32), opposite_slot % slots
+    )
+    back = jnp.take(back, partner, axis=0).astype(F32)
+    here = jnp.where(mom == 0, back[:, 0], back[:, 1])
+    there = jnp.where(mom == 0, back[:, 1], back[:, 0])
+    own_rows = lax.dynamic_slice_in_dim(amplitudes, pts * rows_here, rows_here, 4).astype(F32)
+    gap = cond_energy[:, None, :] - val_energy[:, :, None]
+    result_real = gap * own_rows[0, 0] - here[:, 0]
+    result_imag = gap * own_rows[1, 0] - here[:, 1]
+    anti_real = -gap * own_rows[0, 1] + there[:, 0]
+    anti_imag = -gap * own_rows[1, 1] - there[:, 1]
+    return jnp.stack([jnp.stack([result_real, anti_real]), jnp.stack([result_imag, anti_imag])])
+
+
+CHUNKS = 2
+
+
+def fits(mesh, amplitudes, val_orbitals):
+    groups, holders = mesh.shape["mom"], mesh.shape["pts"]
+    slots = amplitudes.shape[3] // groups
+    points = val_orbitals.shape[3] // (groups * holders)
+    return (
+        groups == 2
+        and holders % 8 == 0
+        and holders & (holders - 1) == 0
+        and slots % (groups * holders) == 0
+        and slots % 128 == 0
+        and points % 16 == 0
+        and amplitudes.shape[2] == 1
+        and amplitudes.shape[4:] == (64, 128)
+        and val_orbitals.shape[3] % (128 * CHUNKS) == 0
+    )
+
+
 def solution(mesh):
     in_specs = (
         P(None, None, None, "mom", None, None),
@@ -113,6 +521,11 @@
         P("mom"),
     )
     out_specs = P(None, None, None, "mom", "pts", None)
-    return jax.shard_map(
-        on_device, mesh=mesh, in_specs=in_specs, out_specs=out_specs, check_vma=False
-    )
+
+    def apply(*arguments):
+        path = fast_path if fits(mesh, *arguments[:2]) else general_path
+        return jax.shard_map(
+            path, mesh=mesh, in_specs=in_specs, out_specs=out_specs, check_vma=False
+        )(*arguments)
+
+    return apply

time: 1020 us -> 361 us (0.35); the launches traced: 1010 us -> 360 us
  matrix products: 246 us -> 0 us
  local copies, waits for them, and re-layouts: 259 us -> 26 us
  blocking collectives: 252 us -> 55.4 us
  Pallas kernels: 0 us -> 136 us
  waiting for transfers between devices: 164 us -> 103 us
  other arithmetic: 61.5 us -> 12.3 us
  starting transfers between devices: 10.2 us -> 27.3 us
  between operations: 13.9 us -> 0.41 us
    dot_general x24 -> x0, matrix products: 246 us -> none  [the longest x4 35.8 us: complex_mix(): jnp.einsum(formula, left[1], right[1], preferred_element_type=jnp.float32)]
    all_to_all x2 -> x1, blocking collectives: 252 us -> 55.4 us  [fast_path(): weighted = lax.all_to_all(send, ('mom', 'pts'), 0, 0, tiled=True)]
    another operation x11 -> x0, local copies, waits for them, and re-layouts: 142 us -> none
    all_to_all x1 -> x2, waiting for transfers between devices: 151 us -> 14.3 us  [the longest x1 14.3 us: fast_path(): back = lax.all_to_all(combined, ('mom', 'pts'), 0, 0, tiled=True)]
    pallas_call x0 -> x4, Pallas kernels: none -> 136 us  [the longest x2 124 us: main_call(): pl.pallas_call(functools.partial(main_body, (own_blocks, block, sizes, po...]
    ppermute x1 -> x21, waiting for transfers between devices: 12.8 us -> 88.5 us  [the longest x3 51.3 us: swap_mom(): return lax.ppermute(value, 'mom', [(0, 1), (1, 0)])]
    all_to_all x3 -> x0, local copies, waits for them, and re-layouts: 58.7 us -> none  [the longest x1 30.2 us: on_device(): lax.all_to_all(jnp.stack([back_real, back_imag]).astype(jnp.bfloat16), 'm...]
    another operation x8 -> x3, other arithmetic: 46.3 us -> 1.44 us  [fast_path(): jnp.stack([jnp.stack([result_real, anti_real]), jnp.stack([result_imag, a...]
  transfers between devices with their start and end apart: 3 -> 23, of which waited for: 2 -> 9; matrix products, arithmetic and copies ran while one was open for 53% -> 7% of each run, Pallas kernels for 0% -> 37%
where the time goes in v1:
time: 361 us; the launch traced here: 360 us
  Pallas kernels  136 us (38%)
  waiting for transfers between devices  103 us (29%)
  blocking collectives  55.4 us (15%)
  starting transfers between devices  27.3 us (8%)
  local copies, waits for them, and re-layouts  26 us (7%)
  other arithmetic  12.3 us (3%)
    pallas_call x2, Pallas kernels, main_call(): pl.pallas_call(functools.partial(main_body, (own_blocks, block, sizes, po...  124 us
    all_to_all x1, blocking collectives, fast_path(): weighted = lax.all_to_all(send, ('mom', 'pts'), 0, 0, tiled=True)  55.4 us
    ppermute x3, waiting for transfers between devices, swap_mom(): return lax.ppermute(value, 'mom', [(0, 1), (1, 0)])  51.3 us
    ppermute x18, waiting for transfers between devices, swap_pts(): lax.ppermute(value, 'pts', [(i, i ^ mask) for i in range(lax.axis_size('p...  37.3 us
    unnamed x42, local copies, waits for them, and re-layouts  16.2 us
    all_to_all x1, waiting for transfers between devices, fast_path(): back = lax.all_to_all(combined, ('mom', 'pts'), 0, 0, tiled=True)  14.3 us
    ppermute x18, starting transfers between devices, swap_pts(): lax.ppermute(value, 'pts', [(i, i ^ mask) for i in range(lax.axis_size('p...  12.7 us
    pallas_call x1, Pallas kernels, half_call(): pl.pallas_call(half_body, out_shape=jax.ShapeDtypeStruct((groups, slots,...  8.61 us
  transfers between devices with their start and end apart: 23, of which 9 were waited for; matrix products, arithmetic and copies ran while one was open for 7% of the time, Pallas kernels for 37%

profile of v1, /device:TPU:0, one launch (start us, length us, event | category | flops | bytes accessed | tf_op | source)
XLA Modules:
  0.0 360.0 jit_solution(11880018463997218518)
XLA Ops:
  0.0 2.9 constant_dynamic-slice_fusion.1
  2.9 3.0 collective-permute-start.11
  5.9 0.0 collective-permute-start.1
  5.9 0.1 add_add_fusion
  6.0 0.1 add.129
  6.1 0.1 select_reduce_fusion
  6.3 0.1 sub.110
  6.4 2.2 gather_fusion
  8.6 3.1 broadcast_select_fusion
  11.7 6.5 %all-to-all-start.1 = ((bf16[32,4,2,32,128]{4,3,2,1,0:T(8,128)(2,1)}), bf16[32,4,2,32,128]{4,3,2,1,0:T(8,128)(2,1)}, u32[]{:S(2)}, u32[]{:S(2)}) async-start(bf16[32,4,2,32,128]{4,3,2,1,0:T(8,128)(2,1)} %broadcast_select_fusion), calls=%async_computation.1 | async-start | bytes 4194304 | tf_op jit(solution)/shard_map/all_to_all | solution.py:451
  18.2 19.2 %collective-permute-done.11.refs_3_ = bf16[2,16,64,256]{3,2,1,0:T(8,128)(2,1)} collective-permute-done((bf16[2,16,64,256]{3,2,1,0:T(8,128)(2,1)S(1)}, bf16[2,16,64,256]{3,2,1,0:T(8,128)(2,1)}, u32[]{:S(2)}, u32[]{:S(2)}) %collective-permute-start.11) | collective-permute-done | bytes 1048608 | tf_op jit(solution)/shard_map/ppermute | solution.py:377
  37.5 0.6 collective-permute-start.13
  38.1 3.4 copy-done
  41.4 8.6 %shard_map.91 = bf16[2,128,2,16,128]{4,3,2,1,0:T(8,128)(2,1)S(1)} custom-call(s32[2]{0:T(128)S(1)} %and_select_fusion.where_ref, bf16[2,2,1,128,64,128]{5,4,3,2,1,0:T(8,128)(2,1)S(1)} %copy-done, bf16[2,128,32,128]{3,2,1,0:T(8,128)(2,1)S(1)} %copy-done.1), custom_call_target="tpu_custom_call" | custom-call | tf_op jit(solution)/shard_map/pallas_call | solution.py:138
  50.0 1.3 slice_bitcast_fusion
  51.4 2.5 collective-permute-start
  53.9 2.1 collective-permute-start.12
  56.0 13.3 %collective-permute-done.1.refs_3_ = bf16[2,16,64,256]{3,2,1,0:T(8,128)(2,1)} collective-permute-done((bf16[2,16,64,256]{3,2,1,0:T(8,128)(2,1)}, bf16[2,16,64,256]{3,2,1,0:T(8,128)(2,1)}, u32[]{:S(2)}, u32[]{:S(2)}) %collective-permute-start.1) | collective-permute-done | bytes 1048608 | tf_op jit(solution)/shard_map/ppermute | solution.py:377
  69.3 2.1 collective-permute-start.2
  71.4 5.8 %collective-permute-done.13.refs_5_ = bf16[2,16,64,256]{3,2,1,0:T(8,128)(2,1)S(1)} collective-permute-done((bf16[2,16,64,256]{3,2,1,0:T(8,128)(2,1)}, bf16[2,16,64,256]{3,2,1,0:T(8,128)(2,1)S(1)}, u32[]{:S(2)}, u32[]{:S(2)}) %collective-permute-start.13) | collective-permute-done | bytes 1048608 | tf_op jit(solution)/shard_map/ppermute | solution.py:381
  77.2 0.6 collective-permute-start.3
  77.8 18.7 %collective-permute-done.refs_1_ = bf16[128,2,16,128]{3,2,1,0:T(8,128)(2,1)S(1)} collective-permute-done((bf16[128,2,16,128]{3,2,1,0:T(8,128)(2,1)S(1)}, bf16[128,2,16,128]{3,2,1,0:T(8,128)(2,1)S(1)}, u32[]{:S(2)}, u32[]{:S(2)}) %collective-permute-start) | collective-permute-done | bytes 1048608 | tf_op jit(solution)/shard_map/ppermute | solution.py:377
  96.5 1.8 collective-permute-start.14
  98.3 10.8 %collective-permute-done.2.refs_4_ = bf16[2,16,64,256]{3,2,1,0:T(8,128)(2,1)S(1)} collective-permute-done((bf16[2,16,64,256]{3,2,1,0:T(8,128)(2,1)}, bf16[2,16,64,256]{3,2,1,0:T(8,128)(2,1)S(1)}, u32[]{:S(2)}, u32[]{:S(2)}) %collective-permute-start.2) | collective-permute-done | bytes 1048608 | tf_op jit(solution)/shard_map/ppermute | solution.py:381
  109.0 0.0 collective-permute-start.18
  109.2 1.4 collective-permute-start.15
  110.5 0.7 collective-permute-start.5
  111.2 1.1 slice.92
  112.3 3.7 %collective-permute-done.14.refs_6_ = bf16[2,8,64,256]{3,2,1,0:T(8,128)(2,1)S(1)} collective-permute-done((bf16[2,8,64,256]{3,2,1,0:T(8,128)(2,1)S(1)}, bf16[2,8,64,256]{3,2,1,0:T(8,128)(2,1)S(1)}, u32[]{:S(2)}, u32[]{:S(2)}) %collective-permute-start.14) | collective-permute-done | bytes 524320 | tf_op jit(solution)/shard_map/ppermute | solution.py:381
  116.0 1.8 collective-permute-start.4
  117.8 6.2 %collective-permute-done.15.refs_7_ = bf16[2,8,64,256]{3,2,1,0:T(8,128)(2,1)S(1)} collective-permute-done((bf16[2,8,64,256]{3,2,1,0:T(8,128)(2,1)S(1)}, bf16[2,8,64,256]{3,2,1,0:T(8,128)(2,1)S(1)}, u32[]{:S(2)}, u32[]{:S(2)}) %collective-permute-start.15) | collective-permute-done | bytes 524320 | tf_op jit(solution)/shard_map/ppermute | solution.py:381
  124.0 10.9 %collective-permute-done.5.refs_7_ = bf16[2,8,64,256]{3,2,1,0:T(8,128)(2,1)} collective-permute-done((bf16[2,8,64,256]{3,2,1,0:T(8,128)(2,1)S(1)}, bf16[2,8,64,256]{3,2,1,0:T(8,128)(2,1)}, u32[]{:S(2)}, u32[]{:S(2)}) %collective-permute-start.5) | collective-permute-done | bytes 524320 | tf_op jit(solution)/shard_map/ppermute | solution.py:381
  134.9 0.5 collective-permute-start.6
  135.4 0.1 collective-permute-start.7
  135.5 0.5 collective-permute-start.8
  136.0 1.2 sine_convert_fusion
  137.3 0.1 collective-permute-start.10
  137.4 0.4 collective-permute-start.9
  137.9 1.1 fusion.15
  139.0 1.0 multiply_bitcast_fusion
  140.0 1.0 copy.20.refs_14_
  141.0 11.4 %copy.36 = bf16[2,256,16,512]{3,1,0,2:T(8,128)(2,1)} copy(bf16[2,256,16,512]{3,2,1,0:T(8,128)(2,1)} %param.12) | data formatting | bytes 16777216 | tf_op args[3]
  152.4 0.7 select_reduce_fusion.1.pos_ref
  153.1 61.5 %shard_map.92.refs_16_ = f32[256,32,128]{2,1,0:T(8,128)} custom-call(s32[8]{0:T(128)} %copy-done.15, s32[256]{0:T(256)} %select_reduce_fusion.1.pos_ref, bf16[128,2,16,128]{3,2,1,0:T(8,128)(2,1)} %get-tuple-element.12.refs_0_, bf16[128,2,16,128]{3,2,1,0:T(8,128)(2,1)} %copy-done.2, bf16[2,128,64,512]{3,2,1,0:T(8,128)(2,1)} %refs_2_.3, ...), custom_call_target="tpu_custom_call" | custom-call | tf_op jit(solution)/shard_map/pallas_call | solution.py:309
  214.7 0.8 copy-done.13
  215.5 62.3 %shard_map.93 = bf16[256,2,16,128]{3,2,1,0:T(8,128)(2,1)} custom-call(s32[8]{0:T(128)} %copy-done.15, s32[256]{0:T(256)} %select_reduce_fusion.1.pos_ref, bf16[128,2,16,128]{3,2,1,0:T(8,128)(2,1)} %get-tuple-element.12.refs_0_, bf16[128,2,16,128]{3,2,1,0:T(8,128)(2,1)} %copy-done.2, bf16[2,128,64,512]{3,2,1,0:T(8,128)(2,1)} %refs_2_.3, ...), custom_call_target="tpu_custom_call" | custom-call | tf_op jit(solution)/shard_map/pallas_call | solution.py:309
  277.8 55.4 %all_to_all.15.weighted_ref = bf16[32,2,4,2,16,128]{5,4,3,2,1,0:T(8,128)(2,1)S(1)} all-to-all(bf16[32,2,4,2,16,128]{5,4,3,2,1,0:T(8,128)(2,1)} %bitcast.69), channel_id=1, replica_groups=mesh['mom'=2,'pts'=16] {'mom','pts'}, dimensions={0} | all-to-all | bytes 4194304 | tf_op jit(solution)/shard_map/all_to_all | solution.py:471
  333.1 3.4 shard_map.94
  336.5 0.8 pad_maximum_fusion
  337.4 2.6 all-to-all-start.2
  340.0 0.1 copy.17
  340.1 1.4 dynamic-slice_convert_fusion
  341.6 14.3 %all-to-all-done.2 = bf16[32,4,2,8,128]{4,3,2,1,0:T(8,128)(2,1)S(1)} async-done(((bf16[32,4,2,8,128]{4,3,2,1,0:T(8,128)(2,1)}), bf16[32,4,2,8,128]{4,3,2,1,0:T(8,128)(2,1)S(1)}, u32[]{:S(2)}, u32[]{:S(2)}) %all-to-all-start.2) | async-done | bytes 524320 | tf_op jit(solution)/shard_map/all_to_all | solution.py:474
  355.8 1.0 gather_fusion.1
  356.9 0.3 select_convert_fusion
  357.2 0.0 copy-start.14
  357.2 0.2 fusion.20
  357.4 0.1 fusion
  357.6 0.4 copy-done.14
  358.0 0.2 fusion.4
  358.2 0.3 fusion.10
  358.6 0.1 maximum_bitcast_fusion.1
  358.7 0.1 maximum_bitcast_fusion.2
  358.8 1.2 maximum_bitcast_fusion
  (68 shorter events, 0.3 us)
Async XLA Ops:
  0.0 5.9 %copy-start.19 = (s32[8]{0:T(128)S(1)}, s32[8]{0:T(128)}, u32[]{:S(2)}) copy-start(s32[8]{0:T(128)} %constant.135.clone) | copy-start | bytes 100
  0.0 6.1 %copy-start.16 = (s32[256]{0:T(256)S(1)}, s32[256]{0:T(256)}, u32[]{:S(2)}) copy-start(s32[256]{0:T(256)} %param.15) | copy-start | bytes 3076
  0.0 6.4 %copy-start.1 = (bf16[2,128,32,128]{3,2,1,0:T(8,128)(2,1)S(1)}, bf16[2,128,32,128]{3,2,1,0:T(8,128)(2,1)}, u32[]{:S(2)}) copy-start(bf16[2,128,32,128]{3,2,1,0:T(8,128)(2,1)} %cond_ref.1) | copy-start | bytes 6291460
  2.9 34.6 %collective-permute-start.11 = (bf16[2,16,64,256]{3,2,1,0:T(8,128)(2,1)S(1)}, bf16[2,16,64,256]{3,2,1,0:T(8,128)(2,1)}, u32[]{:S(2)}, u32[]{:S(2)}) collective-permute-start(bf16[2,16,64,256]{3,2,1,0:T(8,128)(2,1)S(1)} %get-tuple-element.9), channel_id=1, source_target_pairs={{0,16},{16,0},{1,17},{17,1},{2,18},{18,2},{3,19},{19,3},{4,20},{20... | collective-permute-start | bytes 3145736 | tf_op jit(solution)/shard_map/ppermute | solution.py:377
  5.9 63.4 %collective-permute-start.1 = (bf16[2,16,64,256]{3,2,1,0:T(8,128)(2,1)}, bf16[2,16,64,256]{3,2,1,0:T(8,128)(2,1)}, u32[]{:S(2)}, u32[]{:S(2)}) collective-permute-start(bf16[2,16,64,256]{3,2,1,0:T(8,128)(2,1)} %get-tuple-element.10), channel_id=1, source_target_pairs={{0,16},{16,0},{1,17},{17,1},{2,18},{18,2},{3,19},{19,3},{4,20},{20... | collective-permute-start | bytes 3145736 | tf_op jit(solution)/shard_map/ppermute | solution.py:377
  5.9 2.6 copy-start.15
  11.7 266.0 %all-to-all-start.1 = ((bf16[32,4,2,32,128]{4,3,2,1,0:T(8,128)(2,1)}), bf16[32,4,2,32,128]{4,3,2,1,0:T(8,128)(2,1)}, u32[]{:S(2)}, u32[]{:S(2)}) async-start(bf16[32,4,2,32,128]{4,3,2,1,0:T(8,128)(2,1)} %broadcast_select_fusion), calls=%async_computation.1 | async-start | bytes 4194304 | tf_op jit(solution)/shard_map/all_to_all | solution.py:451
  37.5 39.7 %collective-permute-start.13 = (bf16[2,16,64,256]{3,2,1,0:T(8,128)(2,1)}, bf16[2,16,64,256]{3,2,1,0:T(8,128)(2,1)S(1)}, u32[]{:S(2)}, u32[]{:S(2)}) collective-permute-start(bf16[2,16,64,256]{3,2,1,0:T(8,128)(2,1)} %collective-permute-done.11.refs_3_), channel_id=1, source_target_pairs={{0,4},{1,5},{2,6},{3,7},{4,0},{5,1},{6,2},{7,3},{8,12},{9,13},{10,... | collective-permute-start | bytes 3145736 | tf_op jit(solution)/shard_map/ppermute | solution.py:381
  38.0 3.4 copy-start
  51.4 45.1 %collective-permute-start = (bf16[128,2,16,128]{3,2,1,0:T(8,128)(2,1)S(1)}, bf16[128,2,16,128]{3,2,1,0:T(8,128)(2,1)S(1)}, u32[]{:S(2)}, u32[]{:S(2)}) collective-permute-start(bf16[128,2,16,128]{3,2,1,0:T(8,128)(2,1)S(1)} %get-tuple-element.11), channel_id=1, source_target_pairs={{0,16},{16,0},{1,17},{17,1},{2,18},{18,2},{3,19},{19,3},{4,20},{20... | collective-permute-start | bytes 3145736 | tf_op jit(solution)/shard_map/ppermute | solution.py:377
  53.9 44.3 %collective-permute-start.12 = (bf16[2,16,64,256]{3,2,1,0:T(8,128)(2,1)}, bf16[2,16,64,256]{3,2,1,0:T(8,128)(2,1)S(1)}, u32[]{:S(2)}, u32[]{:S(2)}) collective-permute-start(bf16[2,16,64,256]{3,2,1,0:T(8,128)(2,1)} %collective-permute-done.11.refs_3_), channel_id=1, source_target_pairs={{0,2},{1,3},{2,0},{3,1},{4,6},{5,7},{6,4},{7,5},{8,10},{9,11},{10,... | collective-permute-start | bytes 3145736 | tf_op jit(solution)/shard_map/ppermute | solution.py:381
  69.3 39.7 %collective-permute-start.2 = (bf16[2,16,64,256]{3,2,1,0:T(8,128)(2,1)}, bf16[2,16,64,256]{3,2,1,0:T(8,128)(2,1)S(1)}, u32[]{:S(2)}, u32[]{:S(2)}) collective-permute-start(bf16[2,16,64,256]{3,2,1,0:T(8,128)(2,1)} %collective-permute-done.1.refs_3_), channel_id=1, source_target_pairs={{0,2},{1,3},{2,0},{3,1},{4,6},{5,7},{6,4},{7,5},{8,10},{9,11},{10,... | collective-permute-start | bytes 3145736 | tf_op jit(solution)/shard_map/ppermute | solution.py:381
  71.4 37.7 %collective-permute-start.16 = (bf16[2,16,64,256]{3,2,1,0:T(8,128)(2,1)}, bf16[2,16,64,256]{3,2,1,0:T(8,128)(2,1)S(1)}, u32[]{:S(2)}, u32[]{:S(2)}) collective-permute-start(bf16[2,16,64,256]{3,2,1,0:T(8,128)(2,1)} %collective-permute-done.11.refs_3_), channel_id=1, source_target_pairs={{0,1},{1,0},{2,3},{3,2},{4,5},{5,4},{6,7},{7,6},{8,9},{9,8},{10,11... | collective-permute-start | bytes 3145736 | tf_op jit(solution)/shard_map/ppermute | solution.py:381
  77.2 35.2 %copy-start.4 = (bf16[2,16,64,256]{3,2,1,0:T(8,128)(2,1)}, bf16[2,16,64,256]{3,2,1,0:T(8,128)(2,1)S(1)}, u32[]{:S(2)}) copy-start(bf16[2,16,64,256]{3,2,1,0:T(8,128)(2,1)S(1)} %collective-permute-done.13.refs_5_) | copy-start | bytes 3145732
  77.2 33.4 %collective-permute-start.3 = (bf16[2,16,64,256]{3,2,1,0:T(8,128)(2,1)}, bf16[2,16,64,256]{3,2,1,0:T(8,128)(2,1)}, u32[]{:S(2)}, u32[]{:S(2)}) collective-permute-start(bf16[2,16,64,256]{3,2,1,0:T(8,128)(2,1)} %collective-permute-done.1.refs_3_), channel_id=1, source_target_pairs={{0,4},{1,5},{2,6},{3,7},{4,0},{5,1},{6,2},{7,3},{8,12},{9,13},{10,... | collective-permute-start | bytes 3145736 | tf_op jit(solution)/shard_map/ppermute | solution.py:381
  96.5 43.5 %copy-start.2 = (bf16[128,2,16,128]{3,2,1,0:T(8,128)(2,1)}, bf16[128,2,16,128]{3,2,1,0:T(8,128)(2,1)S(1)}, u32[]{:S(2)}) copy-start(bf16[128,2,16,128]{3,2,1,0:T(8,128)(2,1)S(1)} %collective-permute-done.refs_1_) | copy-start | bytes 3145732
  96.5 19.5 %collective-permute-start.14 = (bf16[2,8,64,256]{3,2,1,0:T(8,128)(2,1)S(1)}, bf16[2,8,64,256]{3,2,1,0:T(8,128)(2,1)S(1)}, u32[]{:S(2)}, u32[]{:S(2)}) collective-permute-start(bf16[2,8,64,256]{3,2,1,0:T(8,128)(2,1)S(1)} %slice.94), channel_id=1, source_target_pairs={{0,2},{1,3},{2,0},{3,1},{4,6},{5,7},{6,4},{7,5},{8,10},{9,11},{10,... | collective-permute-start | bytes 1572872 | tf_op jit(solution)/shard_map/ppermute | solution.py:381
  98.2 37.3 %copy-start.5 = (bf16[2,16,64,256]{3,2,1,0:T(8,128)(2,1)}, bf16[2,16,64,256]{3,2,1,0:T(8,128)(2,1)S(1)}, u32[]{:S(2)}) copy-start(bf16[2,16,64,256]{3,2,1,0:T(8,128)(2,1)S(1)} %collective-permute-done.12.refs_4_) | copy-start | bytes 3145732
  98.3 37.2 %collective-permute-start.17 = (bf16[2,16,64,256]{3,2,1,0:T(8,128)(2,1)S(1)}, bf16[2,16,64,256]{3,2,1,0:T(8,128)(2,1)S(1)}, u32[]{:S(2)}, u32[]{:S(2)}) collective-permute-start(bf16[2,16,64,256]{3,2,1,0:T(8,128)(2,1)S(1)} %collective-permute-done.12.refs_4_), channel_id=1, source_target_pairs={{0,1},{1,0},{2,3},{3,2},{4,5},{5,4},{6,7},{7,6},{8,9},{9,8},{10,11... | collective-permute-start | bytes 3145736 | tf_op jit(solution)/shard_map/ppermute | solution.py:381
  109.0 30.9 %copy-start.3 = (bf16[2,16,64,256]{3,2,1,0:T(8,128)(2,1)}, bf16[2,16,64,256]{3,2,1,0:T(8,128)(2,1)S(1)}, u32[]{:S(2)}) copy-start(bf16[2,16,64,256]{3,2,1,0:T(8,128)(2,1)S(1)} %collective-permute-done.2.refs_4_) | copy-start | bytes 3145732
  109.0 26.4 %collective-permute-start.18 = (bf16[2,16,64,256]{3,2,1,0:T(8,128)(2,1)S(1)}, bf16[2,16,64,256]{3,2,1,0:T(8,128)(2,1)S(1)}, u32[]{:S(2)}, u32[]{:S(2)}) collective-permute-start(bf16[2,16,64,256]{3,2,1,0:T(8,128)(2,1)S(1)} %collective-permute-done.13.refs_5_), channel_id=1, source_target_pairs={{0,1},{1,0},{2,3},{3,2},{4,5},{5,4},{6,7},{7,6},{8,9},{9,8},{10,11... | collective-permute-start | bytes 3145736 | tf_op jit(solution)/shard_map/ppermute | solution.py:381
  109.1 29.8 %copy-start.6 = (bf16[2,16,64,256]{3,2,1,0:T(8,128)(2,1)}, bf16[2,16,64,256]{3,2,1,0:T(8,128)(2,1)S(1)}, u32[]{:S(2)}) copy-start(bf16[2,16,64,256]{3,2,1,0:T(8,128)(2,1)S(1)} %collective-permute-done.16.refs_8_) | copy-start | bytes 3145732
  109.2 14.9 %collective-permute-start.15 = (bf16[2,8,64,256]{3,2,1,0:T(8,128)(2,1)S(1)}, bf16[2,8,64,256]{3,2,1,0:T(8,128)(2,1)S(1)}, u32[]{:S(2)}, u32[]{:S(2)}) collective-permute-start(bf16[2,8,64,256]{3,2,1,0:T(8,128)(2,1)S(1)} %slice.95), channel_id=1, source_target_pairs={{0,4},{1,5},{2,6},{3,7},{4,0},{5,1},{6,2},{7,3},{8,12},{9,13},{10,... | collective-permute-start | bytes 1572872 | tf_op jit(solution)/shard_map/ppermute | solution.py:381
  110.5 24.4 %collective-permute-start.5 = (bf16[2,8,64,256]{3,2,1,0:T(8,128)(2,1)S(1)}, bf16[2,8,64,256]{3,2,1,0:T(8,128)(2,1)}, u32[]{:S(2)}, u32[]{:S(2)}) collective-permute-start(bf16[2,8,64,256]{3,2,1,0:T(8,128)(2,1)S(1)} %slice.93), channel_id=1, source_target_pairs={{0,4},{1,5},{2,6},{3,7},{4,0},{5,1},{6,2},{7,3},{8,12},{9,13},{10,... | collective-permute-start | bytes 1572872 | tf_op jit(solution)/shard_map/ppermute | solution.py:381
  116.0 23.0 %copy-start.9 = (bf16[2,8,64,256]{3,2,1,0:T(8,128)(2,1)}, bf16[2,8,64,256]{3,2,1,0:T(8,128)(2,1)S(1)}, u32[]{:S(2)}) copy-start(bf16[2,8,64,256]{3,2,1,0:T(8,128)(2,1)S(1)} %collective-permute-done.14.refs_6_) | copy-start | bytes 1572868
  116.0 18.9 %collective-permute-start.4 = (bf16[2,8,64,256]{3,2,1,0:T(8,128)(2,1)S(1)}, bf16[2,8,64,256]{3,2,1,0:T(8,128)(2,1)}, u32[]{:S(2)}, u32[]{:S(2)}) collective-permute-start(bf16[2,8,64,256]{3,2,1,0:T(8,128)(2,1)S(1)} %slice.92), channel_id=1, source_target_pairs={{0,2},{1,3},{2,0},{3,1},{4,6},{5,7},{6,4},{7,5},{8,10},{9,11},{10,... | collective-permute-start | bytes 1572872 | tf_op jit(solution)/shard_map/ppermute | solution.py:381
  124.0 15.9 %copy-start.10 = (bf16[2,8,64,256]{3,2,1,0:T(8,128)(2,1)}, bf16[2,8,64,256]{3,2,1,0:T(8,128)(2,1)S(1)}, u32[]{:S(2)}) copy-start(bf16[2,8,64,256]{3,2,1,0:T(8,128)(2,1)S(1)} %collective-permute-done.15.refs_7_) | copy-start | bytes 1572868
  124.0 13.2 %collective-permute-start.19 = (bf16[2,8,64,256]{3,2,1,0:T(8,128)(2,1)S(1)}, bf16[2,8,64,256]{3,2,1,0:T(8,128)(2,1)S(1)}, u32[]{:S(2)}, u32[]{:S(2)}) collective-permute-start(bf16[2,8,64,256]{3,2,1,0:T(8,128)(2,1)S(1)} %collective-permute-done.14.refs_6_), channel_id=1, source_target_pairs={{0,1},{1,0},{2,3},{3,2},{4,5},{5,4},{6,7},{7,6},{8,9},{9,8},{10,11... | collective-permute-start | bytes 1572872 | tf_op jit(solution)/shard_map/ppermute | solution.py:381
  134.9 2.5 collective-permute-start.20
  134.9 79.7 %collective-permute-start.6 = (bf16[2,16,64,256]{3,2,1,0:T(8,128)(2,1)}, bf16[2,16,64,256]{3,2,1,0:T(8,128)(2,1)}, u32[]{:S(2)}, u32[]{:S(2)}) collective-permute-start(bf16[2,16,64,256]{3,2,1,0:T(8,128)(2,1)} %collective-permute-done.1.refs_3_), channel_id=1, source_target_pairs={{0,1},{1,0},{2,3},{3,2},{4,5},{5,4},{6,7},{7,6},{8,9},{9,8},{10,11... | collective-permute-start | bytes 3145736 | tf_op jit(solution)/shard_map/ppermute | solution.py:381
  135.4 3.5 copy-start.7
  135.4 79.2 %collective-permute-start.7 = (bf16[2,16,64,256]{3,2,1,0:T(8,128)(2,1)S(1)}, bf16[2,16,64,256]{3,2,1,0:T(8,128)(2,1)}, u32[]{:S(2)}, u32[]{:S(2)}) collective-permute-start(bf16[2,16,64,256]{3,2,1,0:T(8,128)(2,1)S(1)} %collective-permute-done.2.refs_4_), channel_id=1, source_target_pairs={{0,1},{1,0},{2,3},{3,2},{4,5},{5,4},{6,7},{7,6},{8,9},{9,8},{10,11... | collective-permute-start | bytes 3145736 | tf_op jit(solution)/shard_map/ppermute | solution.py:381
  135.5 3.4 copy-start.8
  135.5 79.1 %collective-permute-start.8 = (bf16[2,16,64,256]{3,2,1,0:T(8,128)(2,1)}, bf16[2,16,64,256]{3,2,1,0:T(8,128)(2,1)}, u32[]{:S(2)}, u32[]{:S(2)}) collective-permute-start(bf16[2,16,64,256]{3,2,1,0:T(8,128)(2,1)} %collective-permute-done.3.refs_5_), channel_id=1, source_target_pairs={{0,1},{1,0},{2,3},{3,2},{4,5},{5,4},{6,7},{7,6},{8,9},{9,8},{10,11... | collective-permute-start | bytes 3145736 | tf_op jit(solution)/shard_map/ppermute | solution.py:381
  137.3 1.7 copy-start.11
  137.3 77.4 %collective-permute-start.10 = (bf16[2,8,64,256]{3,2,1,0:T(8,128)(2,1)}, bf16[2,8,64,256]{3,2,1,0:T(8,128)(2,1)S(1)}, u32[]{:S(2)}, u32[]{:S(2)}) collective-permute-start(bf16[2,8,64,256]{3,2,1,0:T(8,128)(2,1)} %collective-permute-done.5.refs_7_), channel_id=1, source_target_pairs={{0,1},{1,0},{2,3},{3,2},{4,5},{5,4},{6,7},{7,6},{8,9},{9,8},{10,11... | collective-permute-start | bytes 1572872 | tf_op jit(solution)/shard_map/ppermute | solution.py:381
  137.4 1.5 copy-start.12
  137.4 77.2 %collective-permute-start.9 = (bf16[2,8,64,256]{3,2,1,0:T(8,128)(2,1)}, bf16[2,8,64,256]{3,2,1,0:T(8,128)(2,1)}, u32[]{:S(2)}, u32[]{:S(2)}) collective-permute-start(bf16[2,8,64,256]{3,2,1,0:T(8,128)(2,1)} %collective-permute-done.4.refs_6_), channel_id=1, source_target_pairs={{0,1},{1,0},{2,3},{3,2},{4,5},{5,4},{6,7},{7,6},{8,9},{9,8},{10,11... | collective-permute-start | bytes 1572872 | tf_op jit(solution)/shard_map/ppermute | solution.py:381
  214.7 0.8 copy-start.13
  333.1 6.9 %copy-start.17 = (f32[128,4]{0,1:T(4,128)S(1)}, f32[128,4]{0,1:T(4,128)}, u32[]{:S(2)}) copy-start(f32[128,4]{0,1:T(4,128)} %param.13) | copy-start | bytes 6148
  333.1 7.0 %copy-start.18 = (s32[128]{0:T(128)S(1)}, s32[128]{0:T(128)}, u32[]{:S(2)}) copy-start(s32[128]{0:T(128)} %param.16) | copy-start | bytes 1540
  337.4 18.5 %all-to-all-start.2 = ((bf16[32,4,2,8,128]{4,3,2,1,0:T(8,128)(2,1)}), bf16[32,4,2,8,128]{4,3,2,1,0:T(8,128)(2,1)S(1)}, u32[]{:S(2)}, u32[]{:S(2)}) async-start(bf16[32,4,2,8,128]{4,3,2,1,0:T(8,128)(2,1)} %pad_maximum_fusion), calls=%async_computation.2 | async-start | bytes 1048576 | tf_op jit(solution)/shard_map/all_to_all | solution.py:474
  357.2 0.8 copy-start.14

commit v2 on v1

--- a/solution.py
+++ b/solution.py
@@ -7,6 +7,7 @@
 from jax.experimental import pallas as pl
 from jax.experimental.pallas import tpu as pltpu
 from jax.sharding import PartitionSpec as P
+
 
 F32 = jnp.float32
 BF16 = jnp.bfloat16
@@ -169,6 +170,7 @@
     blocks = own_blocks + len(groups)
     total = blocks * block
     rows = 4 * points
+    pitch = rows + 1
     lanes = pair_ref.shape[0]
     width = lanes * 128
     step = pl.program_id(0)
@@ -182,14 +184,14 @@
             stacked = jnp.concatenate([half, turned], axis=0)
             val = source[:, kk].reshape(128, width)
             pairs = jnp.dot(stacked, val, preferred_element_type=F32)
-            at = pl.multiple_of((start + kk) * rows, rows)
+            at = (start + kk) * pitch
             for l in range(lanes):
                 pair_ref[l, pl.ds(at, rows), :] = pairs[:, l * 128 : (l + 1) * 128]
 
     def make_weighted(source, half_ref, half_start, start, size):
         for kk in range(size):
             k = start + kk
-            at = pl.multiple_of(k * rows, rows)
+            at = k * pitch
             field = jnp.concatenate(
                 [pair_ref[l, pl.ds(at, rows), :] for l in range(lanes)], axis=1
             ).astype(BF16)
@@ -234,7 +236,7 @@
                 parts = []
                 for ri in range(2):
                     row = ri * 2 * points + b * points + nu
-                    parts.append(pair_ref[l, pl.ds(row, total, stride=rows), :].astype(BF16))
+                    parts.append(pair_ref[l, pl.ds(row, total, stride=pitch), :].astype(BF16))
                 columns.append(jnp.concatenate(parts, axis=0))
             spectrum = jnp.dot(
                 forward_ref[...], jnp.concatenate(columns, axis=1), preferred_element_type=F32
@@ -254,7 +256,7 @@
             for b in range(2):
                 for ri in range(2):
                     row = ri * 2 * points + b * points + nu
-                    pair_ref[l, pl.ds(row, total, stride=rows), :] = field[
+                    pair_ref[l, pl.ds(row, total, stride=pitch), :] = field[
                         ri * total : (ri + 1) * total, b * 128 : (b + 1) * 128
                     ]
 
@@ -306,6 +308,9 @@
         out = jax.ShapeDtypeStruct((total, 2, points, 128), BF16)
     else:
         out = jax.ShapeDtypeStruct((total, 2 * points, 128), F32)
+    columns = 2 * points * width
+    work = 8 * columns * total * total * 2 + 4 * columns * total * 2 * bands * 4
+    traffic = 2 * total * (2 * bands * width * 3 + points * (2 * width + 4 * bands))
     return pl.pallas_call(
         functools.partial(main_body, (own_blocks, block, sizes, points, first, last)),
         out_shape=out,
@@ -314,9 +319,12 @@
             grid=(2 * blocks + points,),
             in_specs=in_specs,
             out_specs=whole(out.shape),
-            scratch_shapes=[pltpu.VMEM((width // 128, total * 4 * points, 128), F32)],
+            scratch_shapes=[pltpu.VMEM((width // 128, total * (4 * points + 1), 128), F32)],
         ),
-        compiler_params=pltpu.CompilerParams(vmem_limit_bytes=60 * MIB),
+        compiler_params=pltpu.CompilerParams(vmem_limit_bytes=62 * MIB),
+        cost_estimate=pl.CostEstimate(
+            flops=work, bytes_accessed=traffic, transcendentals=0
+        ),
     )(base, pos, *operands)
 
 
@@ -381,13 +389,15 @@
     return lax.ppermute(value, "pts", [(i, i ^ mask) for i in range(lax.axis_size("pts"))])
 
 
-def other_val(part):
-    middle = part.shape[1] // 2
-    here = swap_mom(part)
+def gather_chips(here):
+    middle = here.shape[1] // 2
     by_y = swap_pts(here, 2)
     by_z = swap_pts(here, 4)
     across = [swap_pts(by_z[:, :middle], 2), swap_pts(by_y[:, middle:], 4)]
-    groups = [[here], [by_y], [by_z], across]
+    return [[here], [by_y], [by_z], across]
+
+
+def with_cores(groups):
     return groups + [[swap_pts(piece, 1) for piece in group] for group in groups]
 
 
@@ -408,17 +418,18 @@
     rows_here = val_energy.shape[1]
     devices = groups * holders
     pairs = slots // devices
-    points = screened.shape[2]
-    width = val_orbitals.shape[3] // CHUNKS
     eighth = slots // 8
 
     q = pts % 8
     mine = lax.dynamic_slice_in_dim(val_orbitals, q * eighth, eighth, 1)
-    pieces = [other_val(mine[..., c * width : (c + 1) * width]) for c in range(CHUNKS)]
+    size = eighth // STREAMS
+    fetched = [swap_mom(mine[:, c * size : (c + 1) * size]) for c in range(STREAMS)]
 
     where = (jnp.arange(groups, dtype=jnp.int32) - mom) % groups
     halves = half_call(amplitudes, cond_orbitals, where, groups)
-    half_other = swap_mom(halves[1])
+    fetched[-1], half_sent = lax.optimization_barrier((fetched[-1], halves[1]))
+    half_other = swap_mom(half_sent)
+    streams = [gather_chips(here) for here in fetched]
 
     order = q ^ jnp.array([0, 2, 4, 6, 1, 3, 5, 7], dtype=jnp.int32)
     slot_own = mom * slots + jnp.arange(slots, dtype=jnp.int32)
@@ -442,32 +453,39 @@
         [jnp.concatenate([cosine, sine], 1), jnp.concatenate([-sine, cosine], 1)], 0
     )
     backward = forward.T * (1.0 / total)
+    screen = jnp.transpose(screened, (2, 0, 1, 3))
+
+    streams[-1][1], forward, backward, screen, place_here = lax.optimization_barrier(
+        (streams[-1][1], forward, backward, screen, place_here)
+    )
+    streams = [with_cores(stream) for stream in streams]
+    pieces = [sum(groups_of, []) for groups_of in zip(*streams)]
 
     paired = jnp.where(
         mom == 0, jnp.arange(slots, dtype=jnp.int32), opposite[:slots] - slots
     )
     cond_send = jnp.take(jnp.swapaxes(cond_orbitals, 0, 1), paired, axis=0)
     cond_send = cond_send.reshape((devices, pairs) + cond_send.shape[1:])
+    cond_send, pieces, half_other = lax.optimization_barrier(
+        (cond_send, pieces, half_other)
+    )
     cond_pairs = lax.all_to_all(cond_send, ("mom", "pts"), 0, 0, tiled=True)
     cond_pairs = cond_pairs.reshape((groups, holders) + cond_pairs.shape[1:])
 
-    screen = jnp.transpose(screened, (2, 0, 1, 3))
-    summed = None
-    for c in range(CHUNKS):
-        summed = main_call(
-            halves[0],
-            half_other,
-            val_orbitals,
-            c,
-            pieces[c],
-            screen,
-            (forward, backward),
-            order * eighth,
-            place_here,
-            summed,
-            c == CHUNKS - 1,
-        )
-    send = summed.reshape((devices, 2, pairs) + summed.shape[1:])
+    weighted = main_call(
+        halves[0],
+        half_other,
+        val_orbitals,
+        0,
+        pieces,
+        screen,
+        (forward, backward),
+        order * eighth,
+        place_here,
+        None,
+        True,
+    )
+    send = weighted.reshape((devices, 2, pairs) + weighted.shape[1:])
     weighted = lax.all_to_all(send, ("mom", "pts"), 0, 0, tiled=True)
     combined = final_call(weighted, cond_pairs)
     combined = jnp.concatenate([combined, combined], axis=0)
@@ -489,7 +507,7 @@
     return jnp.stack([jnp.stack([result_real, anti_real]), jnp.stack([result_imag, anti_imag])])
 
 
-CHUNKS = 2
+STREAMS = 2
 
 
 def fits(mesh, amplitudes, val_orbitals):
@@ -505,7 +523,8 @@
         and points % 16 == 0
         and amplitudes.shape[2] == 1
         and amplitudes.shape[4:] == (64, 128)
-        and val_orbitals.shape[3] % (128 * CHUNKS) == 0
+        and slots // 8 % (2 * STREAMS) == 0
+        and val_orbitals.shape[3] % 128 == 0
     )
 
 

time: 361 us -> 333 us (0.922)
  Pallas kernels: 136 us -> 82.2 us
  blocking collectives: 55.4 us -> 106 us
  waiting for transfers between devices: 103 us -> 77.6 us
  starting transfers between devices: 27.3 us -> 21.6 us
  local copies, waits for them, and re-layouts: 26 us -> 31.6 us
    pallas_call x2 -> x1, Pallas kernels: 124 us -> 71.7 us  [main_call(): pl.pallas_call(functools.partial(main_body, (own_blocks, block, sizes, po...]
    all_to_all x0 -> x1, blocking collectives: none -> 51.4 us  [fast_path(): cond_pairs = lax.all_to_all(cond_send, ('mom', 'pts'), 0, 0, tiled=True)]
    ppermute x3, waiting for transfers between devices: 51.3 us -> 30.2 us  [swap_mom(): return lax.ppermute(value, 'mom', [(0, 1), (1, 0)])]
    all_to_all x1 -> x0, starting transfers between devices: 6.49 us -> none  [fast_path(): cond_pairs = lax.all_to_all(cond_send, ('mom', 'pts'), 0, 0, tiled=True)]
    ppermute x18, waiting for transfers between devices: 37.3 us -> 33.4 us  [swap_pts(): lax.ppermute(value, 'pts', [(i, i ^ mask) for i in range(lax.axis_size('p...]
    unnamed x42 -> x36, local copies, waits for them, and re-layouts: 16.2 us -> 18.3 us
  transfers between devices with their start and end apart: 23 -> 22, of which waited for: 9 -> 8; matrix products, arithmetic and copies ran while one was open for 7% -> 9% of each run, Pallas kernels for 37% -> 3%
where the time goes in v2:
time: 333 us; the launch traced here: 332 us
  blocking collectives  106 us (32%)
  Pallas kernels  82.2 us (25%)
  waiting for transfers between devices  77.6 us (23%)
  local copies, waits for them, and re-layouts  31.6 us (9%)
  starting transfers between devices  21.6 us (6%)
  other arithmetic  12.4 us (4%)
    pallas_call x1, Pallas kernels, main_call(): pl.pallas_call(functools.partial(main_body, (own_blocks, block, sizes, po...  71.7 us
    all_to_all x1, blocking collectives, fast_path(): weighted = lax.all_to_all(send, ('mom', 'pts'), 0, 0, tiled=True)  55 us
    all_to_all x1, blocking collectives, fast_path(): cond_pairs = lax.all_to_all(cond_send, ('mom', 'pts'), 0, 0, tiled=True)  51.4 us
    ppermute x18, waiting for transfers between devices, swap_pts(): lax.ppermute(value, 'pts', [(i, i ^ mask) for i in range(lax.axis_size('p...  33.4 us
    ppermute x3, waiting for transfers between devices, swap_mom(): return lax.ppermute(value, 'mom', [(0, 1), (1, 0)])  30.2 us
    unnamed x36, local copies, waits for them, and re-layouts  18.3 us
    ppermute x18, starting transfers between devices, swap_pts(): lax.ppermute(value, 'pts', [(i, i ^ mask) for i in range(lax.axis_size('p...  14.2 us
    all_to_all x1, waiting for transfers between devices, fast_path(): back = lax.all_to_all(combined, ('mom', 'pts'), 0, 0, tiled=True)  14 us
  transfers between devices with their start and end apart: 22, of which 8 were waited for; matrix products, arithmetic and copies ran while one was open for 9% of the time, Pallas kernels for 3%

profile of v2, /device:TPU:0, one launch (start us, length us, event | category | flops | bytes accessed | tf_op | source)
XLA Modules:
  0.0 332.2 jit_solution(14070288814937988716)
XLA Ops:
  0.0 2.9 constant_dynamic-slice_fusion.1
  2.9 3.0 collective-permute-start
  5.9 3.4 %copy-done = bf16[2,2,1,128,64,128]{5,4,3,2,1,0:T(8,128)(2,1)S(1)} copy-done((bf16[2,2,1,128,64,128]{5,4,3,2,1,0:T(8,128)(2,1)S(1)}, bf16[2,2,1,128,64,128]{5,4,3,2,1,0:T(8,128)(2,1)}, u32[]{:S(2)}) %copy-start) | copy-done | bytes 8388632
  9.3 8.6 %shard_map.91 = bf16[2,128,2,16,128]{4,3,2,1,0:T(8,128)(2,1)S(1)} custom-call(s32[2]{0:T(128)S(1)} %and_select_fusion.2.where_ref, bf16[2,2,1,128,64,128]{5,4,3,2,1,0:T(8,128)(2,1)S(1)} %copy-done, bf16[2,128,32,128]{3,2,1,0:T(8,128)(2,1)S(1)} %copy-done.1), custom_call_target="tpu_custom_call" | custom-call | tf_op jit(solution)/shard_map/pallas_call | solution.py:139
  17.9 1.7 slice_bitcast_fusion
  19.6 10.6 %collective-permute-done.refs_4_ = bf16[2,8,64,512]{3,2,1,0:T(8,128)(2,1)} collective-permute-done((bf16[2,8,64,512]{3,2,1,0:T(8,128)(2,1)}, bf16[2,8,64,512]{3,2,1,0:T(8,128)(2,1)}, u32[]{:S(2)}, u32[]{:S(2)}) %collective-permute-start) | collective-permute-done | bytes 1048608 | tf_op jit(solution)/shard_map/ppermute | solution.py:385
  30.2 2.1 collective-permute-start.1
  32.2 19.6 %collective-permute-done.2.refs_3_ = bf16[2,8,64,512]{3,2,1,0:T(8,128)(2,1)} collective-permute-done((bf16[2,8,64,512]{3,2,1,0:T(8,128)(2,1)S(1)}, bf16[2,8,64,512]{3,2,1,0:T(8,128)(2,1)}, u32[]{:S(2)}, u32[]{:S(2)}) %collective-permute-start.2) | collective-permute-done | bytes 1048608 | tf_op jit(solution)/shard_map/ppermute | solution.py:385
  51.8 1.8 collective-permute-start.4
  53.6 1.5 collective-permute-start.3
  55.1 0.1 add_add_fusion
  55.2 0.1 add.131
  55.3 11.5 %copy.34 = bf16[2,256,16,512]{3,1,0,2:T(8,128)(2,1)} copy(bf16[2,256,16,512]{3,2,1,0:T(8,128)(2,1)} %param.12) | data formatting | bytes 16777216 | tf_op args[3]
  66.8 0.1 select_reduce_fusion.1
  66.9 0.5 collective-permute-start.5
  67.5 1.6 collective-permute-start.20
  69.0 9.1 %collective-permute-done.4.refs_7_ = bf16[2,8,64,512]{3,2,1,0:T(8,128)(2,1)} collective-permute-done((bf16[2,8,64,512]{3,2,1,0:T(8,128)(2,1)}, bf16[2,8,64,512]{3,2,1,0:T(8,128)(2,1)}, u32[]{:S(2)}, u32[]{:S(2)}) %collective-permute-start.4) | collective-permute-done | bytes 1048608 | tf_op jit(solution)/shard_map/ppermute | solution.py:389
  78.2 0.7 select_reduce_fusion
  78.9 1.1 slice.91
  80.0 1.8 collective-permute-start.6
  81.8 1.1 fusion.15
  82.9 1.3 sine_convert_fusion
  84.2 0.9 multiply_bitcast_fusion
  85.1 1.1 slice.92
  86.2 12.7 %collective-permute-done.5.refs_8_ = bf16[2,8,64,512]{3,2,1,0:T(8,128)(2,1)} collective-permute-done((bf16[2,8,64,512]{3,2,1,0:T(8,128)(2,1)}, bf16[2,8,64,512]{3,2,1,0:T(8,128)(2,1)}, u32[]{:S(2)}, u32[]{:S(2)}) %collective-permute-start.5) | collective-permute-done | bytes 1048608 | tf_op jit(solution)/shard_map/ppermute | solution.py:389
  98.9 1.5 collective-permute-start.7
  100.5 0.5 collective-permute-start.13
  101.0 0.6 copy-done.9
  101.5 0.5 collective-permute-start.14
  102.0 1.1 slice.93
  103.1 0.8 copy-done.12
  103.9 1.5 collective-permute-start.8
  105.4 1.1 slice.94
  106.5 4.6 %collective-permute-done.7.refs_10_ = bf16[2,4,64,512]{3,2,1,0:T(8,128)(2,1)S(1)} collective-permute-done((bf16[2,4,64,512]{3,2,1,0:T(8,128)(2,1)S(1)}, bf16[2,4,64,512]{3,2,1,0:T(8,128)(2,1)S(1)}, u32[]{:S(2)}, u32[]{:S(2)}) %collective-permute-start.7) | collective-permute-done | bytes 524320 | tf_op jit(solution)/shard_map/ppermute | solution.py:389
  111.1 1.4 collective-permute-start.9
  112.5 5.6 %collective-permute-done.8.refs_11_ = bf16[2,4,64,512]{3,2,1,0:T(8,128)(2,1)S(1)} collective-permute-done((bf16[2,4,64,512]{3,2,1,0:T(8,128)(2,1)S(1)}, bf16[2,4,64,512]{3,2,1,0:T(8,128)(2,1)S(1)}, u32[]{:S(2)}, u32[]{:S(2)}) %collective-permute-start.8) | collective-permute-done | bytes 524320 | tf_op jit(solution)/shard_map/ppermute | solution.py:389
  118.1 0.8 copy-done.14
  118.9 0.1 sub.110
  119.0 2.2 gather_fusion
  121.2 1.4 collective-permute-done.9.refs_12_
  122.6 0.5 collective-permute-start.17
  123.2 0.4 collective-permute-start.19
  123.7 3.2 broadcast_select_fusion
  126.9 1.0 copy.18.refs_24_
  127.9 0.7 copy-done.15
  128.7 71.7 %shard_map.92 = bf16[256,2,16,128]{3,2,1,0:T(8,128)(2,1)} custom-call(s32[8]{0:T(128)} %copy-done.7, s32[256]{0:T(256)} %get-tuple-element.35.pos_ref, bf16[128,2,16,128]{3,2,1,0:T(8,128)(2,1)} %get-tuple-element.69.refs_0_, bf16[128,2,16,128]{3,2,1,0:T(8,128)(2,1)} %copy-done.10, bf16[2,128,64,512]{3,2,1,0:T(8,128)(2,1)} %refs_2_.1, ...), custom_call_target="tpu_custom_call" | custom-call | flops 25769803776 | bytes 111149056 | tf_op jit(solution)/shard_map/pallas_call | solution.py:314
  200.4 55.0 %all_to_all.15.weighted_ref = bf16[32,2,4,2,16,128]{5,4,3,2,1,0:T(8,128)(2,1)S(1)} all-to-all(bf16[32,2,4,2,16,128]{5,4,3,2,1,0:T(8,128)(2,1)} %bitcast.70), channel_id=1, replica_groups=mesh['mom'=2,'pts'=16] {'mom','pts'}, dimensions={0} | all-to-all | bytes 4194304 | tf_op jit(solution)/shard_map/all_to_all | solution.py:489
  255.4 51.4 %all_to_all.16 = bf16[32,4,2,32,128]{4,3,2,1,0:T(8,128)(2,1)S(1)} all-to-all(bf16[32,4,2,32,128]{4,3,2,1,0:T(8,128)(2,1)S(1)} %copy-done.2), channel_id=1, replica_groups=mesh['mom'=2,'pts'=16] {'mom','pts'}, dimensions={0} | all-to-all | bytes 4194304 | tf_op jit(solution)/shard_map/all_to_all | solution.py:472
  306.8 1.8 shard_map.93
  308.7 0.8 pad_maximum_fusion
  309.5 2.8 all-to-all-start.2
  312.3 0.1 copy.16
  312.5 1.4 dynamic-slice_convert_fusion
  313.9 14.0 %all-to-all-done.2 = bf16[32,4,2,8,128]{4,3,2,1,0:T(8,128)(2,1)S(1)} async-done(((bf16[32,4,2,8,128]{4,3,2,1,0:T(8,128)(2,1)}), bf16[32,4,2,8,128]{4,3,2,1,0:T(8,128)(2,1)S(1)}, u32[]{:S(2)}, u32[]{:S(2)}) %all-to-all-start.2) | async-done | bytes 524320 | tf_op jit(solution)/shard_map/all_to_all | solution.py:492
  328.0 1.0 gather_fusion.1
  329.0 0.3 select_convert_fusion
  329.3 0.2 fusion.20
  329.6 0.1 fusion
  329.7 0.4 copy-done.4
  330.2 0.2 fusion.4
  330.4 0.3 fusion.10
  330.7 0.1 maximum_bitcast_fusion.2
  330.8 0.1 maximum_bitcast_fusion.1
  330.9 1.2 maximum_bitcast_fusion
  (59 shorter events, 0.3 us)
Async XLA Ops:
  0.0 5.9 %copy-start.1 = (bf16[2,128,32,128]{3,2,1,0:T(8,128)(2,1)S(1)}, bf16[2,128,32,128]{3,2,1,0:T(8,128)(2,1)}, u32[]{:S(2)}) copy-start(bf16[2,128,32,128]{3,2,1,0:T(8,128)(2,1)} %cond_ref.1) | copy-start | bytes 6291460
  2.9 27.3 %collective-permute-start = (bf16[2,8,64,512]{3,2,1,0:T(8,128)(2,1)}, bf16[2,8,64,512]{3,2,1,0:T(8,128)(2,1)}, u32[]{:S(2)}, u32[]{:S(2)}) collective-permute-start(bf16[2,8,64,512]{3,2,1,0:T(8,128)(2,1)} %get-tuple-element.68), channel_id=1, source_target_pairs={{0,16},{16,0},{1,17},{17,1},{2,18},{18,2},{3,19},{19,3},{4,20},{20... | collective-permute-start | bytes 3145736 | tf_op jit(solution)/shard_map/ppermute | solution.py:385
  5.8 45.9 %collective-permute-start.2 = (bf16[2,8,64,512]{3,2,1,0:T(8,128)(2,1)S(1)}, bf16[2,8,64,512]{3,2,1,0:T(8,128)(2,1)}, u32[]{:S(2)}, u32[]{:S(2)}) collective-permute-start(bf16[2,8,64,512]{3,2,1,0:T(8,128)(2,1)S(1)} %get-tuple-element.67), channel_id=1, source_target_pairs={{0,16},{16,0},{1,17},{17,1},{2,18},{18,2},{3,19},{19,3},{4,20},{20... | collective-permute-start | bytes 3145736 | tf_op jit(solution)/shard_map/ppermute | solution.py:385
  5.9 3.4 %copy-start = (bf16[2,2,1,128,64,128]{5,4,3,2,1,0:T(8,128)(2,1)S(1)}, bf16[2,2,1,128,64,128]{5,4,3,2,1,0:T(8,128)(2,1)}, u32[]{:S(2)}) copy-start(bf16[2,2,1,128,64,128]{5,4,3,2,1,0:T(8,128)(2,1)} %amp_ref.1) | copy-start | bytes 25165828
  17.9 37.3 %copy-start.16 = (s32[8]{0:T(128)S(1)}, s32[8]{0:T(128)}, u32[]{:S(2)}) copy-start(s32[8]{0:T(128)} %constant.135.clone) | copy-start | bytes 100
  30.2 37.3 %collective-permute-start.1 = (bf16[2,8,64,512]{3,2,1,0:T(8,128)(2,1)}, bf16[2,8,64,512]{3,2,1,0:T(8,128)(2,1)}, u32[]{:S(2)}, u32[]{:S(2)}) collective-permute-start(bf16[2,8,64,512]{3,2,1,0:T(8,128)(2,1)} %collective-permute-done.refs_4_), channel_id=1, source_target_pairs={{0,2},{1,3},{2,0},{3,1},{4,6},{5,7},{6,4},{7,5},{8,10},{9,11},{10,... | collective-permute-start | bytes 3145736 | tf_op jit(solution)/shard_map/ppermute | solution.py:389
  51.8 26.3 %collective-permute-start.4 = (bf16[2,8,64,512]{3,2,1,0:T(8,128)(2,1)}, bf16[2,8,64,512]{3,2,1,0:T(8,128)(2,1)}, u32[]{:S(2)}, u32[]{:S(2)}) collective-permute-start(bf16[2,8,64,512]{3,2,1,0:T(8,128)(2,1)} %collective-permute-done.2.refs_3_), channel_id=1, source_target_pairs={{0,4},{1,5},{2,6},{3,7},{4,0},{5,1},{6,2},{7,3},{8,12},{9,13},{10,... | collective-permute-start | bytes 3145736 | tf_op jit(solution)/shard_map/ppermute | solution.py:389
  53.6 26.4 %collective-permute-start.3 = (bf16[2,8,64,512]{3,2,1,0:T(8,128)(2,1)}, bf16[2,8,64,512]{3,2,1,0:T(8,128)(2,1)}, u32[]{:S(2)}, u32[]{:S(2)}) collective-permute-start(bf16[2,8,64,512]{3,2,1,0:T(8,128)(2,1)} %collective-permute-done.2.refs_3_), channel_id=1, source_target_pairs={{0,2},{1,3},{2,0},{3,1},{4,6},{5,7},{6,4},{7,5},{8,10},{9,11},{10,... | collective-permute-start | bytes 3145736 | tf_op jit(solution)/shard_map/ppermute | solution.py:389
  55.1 11.7 %copy-start.7 = (s32[8]{0:T(128)}, s32[8]{0:T(128)S(1)}, u32[]{:S(2)}) copy-start(s32[8]{0:T(128)S(1)} %xor_multiply_fusion.base_ref) | copy-start | bytes 100
  55.3 11.5 %copy-start.5 = (s32[256]{0:T(256)S(1)}, s32[256]{0:T(256)}, u32[]{:S(2)}) copy-start(s32[256]{0:T(256)} %param.15) | copy-start | bytes 3076
  55.3 12.2 %copy-start.3 = (bf16[128,2,16,128]{3,2,1,0:T(8,128)(2,1)S(1)}, bf16[128,2,16,128]{3,2,1,0:T(8,128)(2,1)}, u32[]{:S(2)}) copy-start(bf16[128,2,16,128]{3,2,1,0:T(8,128)(2,1)} %get-tuple-element.37) | copy-start | bytes 3145732
  66.9 32.0 %collective-permute-start.5 = (bf16[2,8,64,512]{3,2,1,0:T(8,128)(2,1)}, bf16[2,8,64,512]{3,2,1,0:T(8,128)(2,1)}, u32[]{:S(2)}, u32[]{:S(2)}) collective-permute-start(bf16[2,8,64,512]{3,2,1,0:T(8,128)(2,1)} %collective-permute-done.refs_4_), channel_id=1, source_target_pairs={{0,4},{1,5},{2,6},{3,7},{4,0},{5,1},{6,2},{7,3},{8,12},{9,13},{10,... | collective-permute-start | bytes 3145736 | tf_op jit(solution)/shard_map/ppermute | solution.py:389
  67.4 33.0 %collective-permute-start.11 = (bf16[2,8,64,512]{3,2,1,0:T(8,128)(2,1)}, bf16[2,8,64,512]{3,2,1,0:T(8,128)(2,1)S(1)}, u32[]{:S(2)}, u32[]{:S(2)}) collective-permute-start(bf16[2,8,64,512]{3,2,1,0:T(8,128)(2,1)} %collective-permute-done.refs_4_), channel_id=1, source_target_pairs={{0,1},{1,0},{2,3},{3,2},{4,5},{5,4},{6,7},{7,6},{8,9},{9,8},{10,11... | collective-permute-start | bytes 3145736 | tf_op jit(solution)/shard_map/ppermute | solution.py:389
  67.5 33.5 %collective-permute-start.20 = (bf16[128,2,16,128]{3,2,1,0:T(8,128)(2,1)S(1)}, bf16[128,2,16,128]{3,2,1,0:T(8,128)(2,1)S(1)}, u32[]{:S(2)}, u32[]{:S(2)}) collective-permute-start(bf16[128,2,16,128]{3,2,1,0:T(8,128)(2,1)S(1)} %copy-done.3), channel_id=1, source_target_pairs={{0,16},{16,0},{1,17},{17,1},{2,18},{18,2},{3,19},{19,3},{4,20},{20... | collective-permute-start | bytes 3145736 | tf_op jit(solution)/shard_map/ppermute | solution.py:385
  78.1 22.3 %collective-permute-start.10 = (bf16[2,8,64,512]{3,2,1,0:T(8,128)(2,1)}, bf16[2,8,64,512]{3,2,1,0:T(8,128)(2,1)S(1)}, u32[]{:S(2)}, u32[]{:S(2)}) collective-permute-start(bf16[2,8,64,512]{3,2,1,0:T(8,128)(2,1)} %collective-permute-done.2.refs_3_), channel_id=1, source_target_pairs={{0,1},{1,0},{2,3},{3,2},{4,5},{5,4},{6,7},{7,6},{8,9},{9,8},{10,11... | collective-permute-start | bytes 3145736 | tf_op jit(solution)/shard_map/ppermute | solution.py:389
  80.0 23.1 %collective-permute-start.6 = (bf16[2,4,64,512]{3,2,1,0:T(8,128)(2,1)S(1)}, bf16[2,4,64,512]{3,2,1,0:T(8,128)(2,1)S(1)}, u32[]{:S(2)}, u32[]{:S(2)}) collective-permute-start(bf16[2,4,64,512]{3,2,1,0:T(8,128)(2,1)S(1)} %slice.91), channel_id=1, source_target_pairs={{0,2},{1,3},{2,0},{3,1},{4,6},{5,7},{6,4},{7,5},{8,10},{9,11},{10,... | collective-permute-start | bytes 1572872 | tf_op jit(solution)/shard_map/ppermute | solution.py:389
  98.9 12.2 %collective-permute-start.7 = (bf16[2,4,64,512]{3,2,1,0:T(8,128)(2,1)S(1)}, bf16[2,4,64,512]{3,2,1,0:T(8,128)(2,1)S(1)}, u32[]{:S(2)}, u32[]{:S(2)}) collective-permute-start(bf16[2,4,64,512]{3,2,1,0:T(8,128)(2,1)S(1)} %slice.92), channel_id=1, source_target_pairs={{0,4},{1,5},{2,6},{3,7},{4,0},{5,1},{6,2},{7,3},{8,12},{9,13},{10,... | collective-permute-start | bytes 1572872 | tf_op jit(solution)/shard_map/ppermute | solution.py:389
  100.4 17.7 %copy-start.11 = (bf16[2,8,64,512]{3,2,1,0:T(8,128)(2,1)}, bf16[2,8,64,512]{3,2,1,0:T(8,128)(2,1)S(1)}, u32[]{:S(2)}) copy-start(bf16[2,8,64,512]{3,2,1,0:T(8,128)(2,1)S(1)} %collective-permute-done.10.refs_13_) | copy-start | bytes 3145732
  100.4 22.2 %collective-permute-start.12 = (bf16[2,8,64,512]{3,2,1,0:T(8,128)(2,1)}, bf16[2,8,64,512]{3,2,1,0:T(8,128)(2,1)}, u32[]{:S(2)}, u32[]{:S(2)}) collective-permute-start(bf16[2,8,64,512]{3,2,1,0:T(8,128)(2,1)} %collective-permute-done.3.refs_5_), channel_id=1, source_target_pairs={{0,1},{1,0},{2,3},{3,2},{4,5},{5,4},{6,7},{7,6},{8,9},{9,8},{10,11... | collective-permute-start | bytes 3145736 | tf_op jit(solution)/shard_map/ppermute | solution.py:389
  100.5 1.1 copy-start.9
  100.5 22.7 %collective-permute-start.13 = (bf16[2,8,64,512]{3,2,1,0:T(8,128)(2,1)}, bf16[2,8,64,512]{3,2,1,0:T(8,128)(2,1)}, u32[]{:S(2)}, u32[]{:S(2)}) collective-permute-start(bf16[2,8,64,512]{3,2,1,0:T(8,128)(2,1)} %collective-permute-done.1.refs_6_), channel_id=1, source_target_pairs={{0,1},{1,0},{2,3},{3,2},{4,5},{5,4},{6,7},{7,6},{8,9},{9,8},{10,11... | collective-permute-start | bytes 3145736 | tf_op jit(solution)/shard_map/ppermute | solution.py:389
  101.5 16.6 %copy-start.10 = (bf16[128,2,16,128]{3,2,1,0:T(8,128)(2,1)}, bf16[128,2,16,128]{3,2,1,0:T(8,128)(2,1)S(1)}, u32[]{:S(2)}) copy-start(bf16[128,2,16,128]{3,2,1,0:T(8,128)(2,1)S(1)} %collective-permute-done.20.refs_1_) | copy-start | bytes 3145732
  101.5 21.7 %collective-permute-start.14 = (bf16[2,8,64,512]{3,2,1,0:T(8,128)(2,1)}, bf16[2,8,64,512]{3,2,1,0:T(8,128)(2,1)}, u32[]{:S(2)}, u32[]{:S(2)}) collective-permute-start(bf16[2,8,64,512]{3,2,1,0:T(8,128)(2,1)} %collective-permute-done.4.refs_7_), channel_id=1, source_target_pairs={{0,1},{1,0},{2,3},{3,2},{4,5},{5,4},{6,7},{7,6},{8,9},{9,8},{10,11... | collective-permute-start | bytes 3145736 | tf_op jit(solution)/shard_map/ppermute | solution.py:389
  103.1 0.8 copy-start.12
  103.9 14.2 %collective-permute-start.8 = (bf16[2,4,64,512]{3,2,1,0:T(8,128)(2,1)S(1)}, bf16[2,4,64,512]{3,2,1,0:T(8,128)(2,1)S(1)}, u32[]{:S(2)}, u32[]{:S(2)}) collective-permute-start(bf16[2,4,64,512]{3,2,1,0:T(8,128)(2,1)S(1)} %slice.93), channel_id=1, source_target_pairs={{0,2},{1,3},{2,0},{3,1},{4,6},{5,7},{6,4},{7,5},{8,10},{9,11},{10,... | collective-permute-start | bytes 1572872 | tf_op jit(solution)/shard_map/ppermute | solution.py:389
  111.1 7.0 %copy-start.13 = (bf16[2,4,64,512]{3,2,1,0:T(8,128)(2,1)}, bf16[2,4,64,512]{3,2,1,0:T(8,128)(2,1)S(1)}, u32[]{:S(2)}) copy-start(bf16[2,4,64,512]{3,2,1,0:T(8,128)(2,1)S(1)} %collective-permute-done.7.refs_10_) | copy-start | bytes 1572868
  111.1 11.5 %collective-permute-start.9 = (bf16[2,4,64,512]{3,2,1,0:T(8,128)(2,1)S(1)}, bf16[2,4,64,512]{3,2,1,0:T(8,128)(2,1)}, u32[]{:S(2)}, u32[]{:S(2)}) collective-permute-start(bf16[2,4,64,512]{3,2,1,0:T(8,128)(2,1)S(1)} %slice.94), channel_id=1, source_target_pairs={{0,4},{1,5},{2,6},{3,7},{4,0},{5,1},{6,2},{7,3},{8,12},{9,13},{10,... | collective-permute-start | bytes 1572872 | tf_op jit(solution)/shard_map/ppermute | solution.py:389
  118.1 0.8 copy-start.14
  118.9 9.0 %collective-permute-start.15 = (bf16[2,8,64,512]{3,2,1,0:T(8,128)(2,1)}, bf16[2,8,64,512]{3,2,1,0:T(8,128)(2,1)}, u32[]{:S(2)}, u32[]{:S(2)}) collective-permute-start(bf16[2,8,64,512]{3,2,1,0:T(8,128)(2,1)} %collective-permute-done.5.refs_8_), channel_id=1, source_target_pairs={{0,1},{1,0},{2,3},{3,2},{4,5},{5,4},{6,7},{7,6},{8,9},{9,8},{10,11... | collective-permute-start | bytes 3145736 | tf_op jit(solution)/shard_map/ppermute | solution.py:389
  122.6 5.3 %collective-permute-start.16 = (bf16[2,4,64,512]{3,2,1,0:T(8,128)(2,1)}, bf16[2,4,64,512]{3,2,1,0:T(8,128)(2,1)S(1)}, u32[]{:S(2)}, u32[]{:S(2)}) collective-permute-start(bf16[2,4,64,512]{3,2,1,0:T(8,128)(2,1)} %copy-done.12), channel_id=1, source_target_pairs={{0,1},{1,0},{2,3},{3,2},{4,5},{5,4},{6,7},{7,6},{8,9},{9,8},{10,11... | collective-permute-start | bytes 1572872 | tf_op jit(solution)/shard_map/ppermute | solution.py:389
  122.6 5.3 %collective-permute-start.17 = (bf16[2,4,64,512]{3,2,1,0:T(8,128)(2,1)}, bf16[2,4,64,512]{3,2,1,0:T(8,128)(2,1)}, u32[]{:S(2)}, u32[]{:S(2)}) collective-permute-start(bf16[2,4,64,512]{3,2,1,0:T(8,128)(2,1)} %copy-done.13), channel_id=1, source_target_pairs={{0,1},{1,0},{2,3},{3,2},{4,5},{5,4},{6,7},{7,6},{8,9},{9,8},{10,11... | collective-permute-start | bytes 1572872 | tf_op jit(solution)/shard_map/ppermute | solution.py:389
  123.1 4.8 %collective-permute-start.18 = (bf16[2,4,64,512]{3,2,1,0:T(8,128)(2,1)}, bf16[2,4,64,512]{3,2,1,0:T(8,128)(2,1)}, u32[]{:S(2)}, u32[]{:S(2)}) collective-permute-start(bf16[2,4,64,512]{3,2,1,0:T(8,128)(2,1)} %copy-done.14), channel_id=1, source_target_pairs={{0,1},{1,0},{2,3},{3,2},{4,5},{5,4},{6,7},{7,6},{8,9},{9,8},{10,11... | collective-permute-start | bytes 1572872 | tf_op jit(solution)/shard_map/ppermute | solution.py:389
  123.2 4.7 %collective-permute-start.19 = (bf16[2,4,64,512]{3,2,1,0:T(8,128)(2,1)}, bf16[2,4,64,512]{3,2,1,0:T(8,128)(2,1)}, u32[]{:S(2)}, u32[]{:S(2)}) collective-permute-start(bf16[2,4,64,512]{3,2,1,0:T(8,128)(2,1)} %collective-permute-done.9.refs_12_), channel_id=1, source_target_pairs={{0,1},{1,0},{2,3},{3,2},{4,5},{5,4},{6,7},{7,6},{8,9},{9,8},{10,11... | collective-permute-start | bytes 1572872 | tf_op jit(solution)/shard_map/ppermute | solution.py:389
  127.9 0.8 copy-start.15
  200.4 55.1 %copy-start.2 = (bf16[32,4,2,32,128]{4,3,2,1,0:T(8,128)(2,1)S(1)}, bf16[32,4,2,32,128]{4,3,2,1,0:T(8,128)(2,1)}, u32[]{:S(2)}) copy-start(bf16[32,4,2,32,128]{4,3,2,1,0:T(8,128)(2,1)} %broadcast_select_fusion) | copy-start | bytes 6291460
  306.8 5.5 %copy-start.6 = (f32[128,4]{0,1:T(4,128)S(1)}, f32[128,4]{0,1:T(4,128)}, u32[]{:S(2)}) copy-start(f32[128,4]{0,1:T(4,128)} %param.13) | copy-start | bytes 6148
  306.8 5.6 %copy-start.8 = (s32[128]{0:T(128)S(1)}, s32[128]{0:T(128)}, u32[]{:S(2)}) copy-start(s32[128]{0:T(128)} %param.16) | copy-start | bytes 1540
  309.5 18.5 %all-to-all-start.2 = ((bf16[32,4,2,8,128]{4,3,2,1,0:T(8,128)(2,1)}), bf16[32,4,2,8,128]{4,3,2,1,0:T(8,128)(2,1)S(1)}, u32[]{:S(2)}, u32[]{:S(2)}) async-start(bf16[32,4,2,8,128]{4,3,2,1,0:T(8,128)(2,1)} %pad_maximum_fusion), calls=%async_computation.2 | async-start | bytes 1048576 | tf_op jit(solution)/shard_map/all_to_all | solution.py:492
  329.3 0.8 copy-start.4

commit v3 on v2

--- a/solution.py
+++ b/solution.py
@@ -427,9 +427,12 @@
 
     where = (jnp.arange(groups, dtype=jnp.int32) - mom) % groups
     halves = half_call(amplitudes, cond_orbitals, where, groups)
-    fetched[-1], half_sent = lax.optimization_barrier((fetched[-1], halves[1]))
-    half_other = swap_mom(half_sent)
-    streams = [gather_chips(here) for here in fetched]
+    screen = jnp.transpose(screened, (2, 0, 1, 3))
+    fetched[-1], half_sent, screen = lax.optimization_barrier(
+        (fetched[-1], halves[1], screen)
+    )
+    streams = [with_cores(gather_chips(here)) for here in fetched]
+    pieces = [sum(groups_of, []) for groups_of in zip(*streams)]
 
     order = q ^ jnp.array([0, 2, 4, 6, 1, 3, 5, 7], dtype=jnp.int32)
     slot_own = mom * slots + jnp.arange(slots, dtype=jnp.int32)
@@ -452,20 +455,23 @@
     forward = jnp.concatenate(
         [jnp.concatenate([cosine, sine], 1), jnp.concatenate([-sine, cosine], 1)], 0
     )
-    backward = forward.T * (1.0 / total)
-    screen = jnp.transpose(screened, (2, 0, 1, 3))
-
-    streams[-1][1], forward, backward, screen, place_here = lax.optimization_barrier(
-        (streams[-1][1], forward, backward, screen, place_here)
-    )
-    streams = [with_cores(stream) for stream in streams]
-    pieces = [sum(groups_of, []) for groups_of in zip(*streams)]
+    turned = grid_here[:, None] * every[None, :] % total
+    turned = turned.astype(F32) * (2.0 * math.pi / total)
+    cosine = jnp.cos(turned).astype(BF16) * (1.0 / total)
+    sine = jnp.sin(turned).astype(BF16) * (1.0 / total)
+    backward = jnp.concatenate(
+        [jnp.concatenate([cosine, -sine], 1), jnp.concatenate([sine, cosine], 1)], 0
+    )
 
     paired = jnp.where(
         mom == 0, jnp.arange(slots, dtype=jnp.int32), opposite[:slots] - slots
     )
-    cond_send = jnp.take(jnp.swapaxes(cond_orbitals, 0, 1), paired, axis=0)
+    cond_send = jnp.take(jnp.swapaxes(cond_orbitals, 0, 1), paired, axis=0, mode="clip")
     cond_send = cond_send.reshape((devices, pairs) + cond_send.shape[1:])
+    half_sent, forward, backward, place_here, cond_send = lax.optimization_barrier(
+        (half_sent, forward, backward, place_here, cond_send)
+    )
+    half_other = swap_mom(half_sent)
     cond_send, pieces, half_other = lax.optimization_barrier(
         (cond_send, pieces, half_other)
     )
@@ -495,7 +501,7 @@
     partner = jnp.where(
         mom == 0, jnp.arange(slots, dtype=jnp.int32), opposite_slot % slots
     )
-    back = jnp.take(back, partner, axis=0).astype(F32)
+    back = jnp.take(back, partner, axis=0, mode="clip").astype(F32)
     here = jnp.where(mom == 0, back[:, 0], back[:, 1])
     there = jnp.where(mom == 0, back[:, 1], back[:, 0])
     own_rows = lax.dynamic_slice_in_dim(amplitudes, pts * rows_here, rows_here, 4).astype(F32)

time: 333 us -> 321 us (0.964)
  waiting for transfers between devices: 77.6 us -> 71.9 us
  local copies, waits for them, and re-layouts: 31.6 us -> 27.7 us
    ppermute x3, waiting for transfers between devices: 30.2 us -> 13 us  [swap_mom(): return lax.ppermute(value, 'mom', [(0, 1), (1, 0)])]
    ppermute x18, waiting for transfers between devices: 33.4 us -> 44.8 us  [swap_pts(): lax.ppermute(value, 'pts', [(i, i ^ mask) for i in range(lax.axis_size('p...]
    unnamed x36 -> x56, local copies, waits for them, and re-layouts: 18.3 us -> 16.5 us
  transfers between devices with their start and end apart: 22 -> 22, of which waited for: 8 -> 11; matrix products, arithmetic and copies ran while one was open for 9% -> 8% of each run, Pallas kernels for 3% -> 3%
where the time goes in v3:
time: 321 us; the launch traced here: 320 us
  blocking collectives  106 us (33%)
  Pallas kernels  82.2 us (26%)
  waiting for transfers between devices  71.9 us (22%)
  local copies, waits for them, and re-layouts  27.7 us (9%)
  starting transfers between devices  20.6 us (6%)
  other arithmetic  11.4 us (4%)
    pallas_call x1, Pallas kernels, main_call(): pl.pallas_call(functools.partial(main_body, (own_blocks, block, sizes, po...  71.8 us
    all_to_all x1, blocking collectives, fast_path(): weighted = lax.all_to_all(send, ('mom', 'pts'), 0, 0, tiled=True)  54.6 us
    all_to_all x1, blocking collectives, fast_path(): cond_pairs = lax.all_to_all(cond_send, ('mom', 'pts'), 0, 0, tiled=True)  51.4 us
    ppermute x18, waiting for transfers between devices, swap_pts(): lax.ppermute(value, 'pts', [(i, i ^ mask) for i in range(lax.axis_size('p...  44.8 us
    unnamed x56, local copies, waits for them, and re-layouts  16.5 us
    all_to_all x1, waiting for transfers between devices, fast_path(): back = lax.all_to_all(combined, ('mom', 'pts'), 0, 0, tiled=True)  14 us
    ppermute x18, starting transfers between devices, swap_pts(): lax.ppermute(value, 'pts', [(i, i ^ mask) for i in range(lax.axis_size('p...  13.3 us
    ppermute x3, waiting for transfers between devices, swap_mom(): return lax.ppermute(value, 'mom', [(0, 1), (1, 0)])  13 us
  transfers between devices with their start and end apart: 22, of which 11 were waited for; matrix products, arithmetic and copies ran while one was open for 8% of the time, Pallas kernels for 3%

profile of v3, /device:TPU:0, one launch (start us, length us, event | category | flops | bytes accessed | tf_op | source)
XLA Modules:
  0.0 320.1 jit_solution(15328574811523071059)
XLA Ops:
  0.0 2.8 constant_dynamic-slice_fusion.1
  2.8 3.0 collective-permute-start
  5.7 0.0 collective-permute-start.1
  5.8 0.1 add_add_fusion
  5.9 11.6 %copy.32 = bf16[2,256,16,512]{3,1,0,2:T(8,128)(2,1)} copy(bf16[2,256,16,512]{3,2,1,0:T(8,128)(2,1)} %param.12) | data formatting | bytes 16777216 | tf_op args[3]
  17.4 0.1 add.115
  17.5 3.4 %copy-done = bf16[2,2,1,128,64,128]{5,4,3,2,1,0:T(8,128)(2,1)S(1)} copy-done((bf16[2,2,1,128,64,128]{5,4,3,2,1,0:T(8,128)(2,1)S(1)}, bf16[2,2,1,128,64,128]{5,4,3,2,1,0:T(8,128)(2,1)}, u32[]{:S(2)}) %copy-start) | copy-done | bytes 8388632
  20.9 8.6 %shard_map.91 = bf16[2,128,2,16,128]{4,3,2,1,0:T(8,128)(2,1)S(1)} custom-call(s32[2]{0:T(128)S(1)} %and_select_fusion.3.where_ref, bf16[2,2,1,128,64,128]{5,4,3,2,1,0:T(8,128)(2,1)S(1)} %copy-done, bf16[2,128,32,128]{3,2,1,0:T(8,128)(2,1)S(1)} %copy-done.1), custom_call_target="tpu_custom_call" | custom-call | tf_op jit(solution)/shard_map/pallas_call | solution.py:139
  29.6 0.2 select_reduce_fusion.1
  29.8 0.8 select_reduce_fusion
  30.5 1.7 slice_bitcast_fusion
  32.2 2.1 collective-permute-start.5
  34.3 1.5 collective-permute-start.3
  35.8 2.9 fusion.23
  38.7 13.0 %collective-permute-done.1.refs_3_ = bf16[2,8,64,512]{3,2,1,0:T(8,128)(2,1)} collective-permute-done((bf16[2,8,64,512]{3,2,1,0:T(8,128)(2,1)S(1)}, bf16[2,8,64,512]{3,2,1,0:T(8,128)(2,1)}, u32[]{:S(2)}, u32[]{:S(2)}) %collective-permute-start.1) | collective-permute-done | bytes 1048608 | tf_op jit(solution)/shard_map/ppermute | solution.py:385
  51.7 1.8 collective-permute-start.4
  53.5 2.1 gather_fusion
  55.7 0.8 maximum_maximum_fusion.1.refs_25_
  56.5 1.1 sine_convert_fusion.1
  57.6 0.9 maximum_maximum_fusion.refs_24_
  58.5 1.5 collective-permute-start.20
  60.0 1.5 collective-permute-start.2
  61.5 0.2 collective-permute-start.10
  61.7 1.1 slice.87
  62.8 16.9 %collective-permute-done.4.refs_7_ = bf16[2,8,64,512]{3,2,1,0:T(8,128)(2,1)} collective-permute-done((bf16[2,8,64,512]{3,2,1,0:T(8,128)(2,1)}, bf16[2,8,64,512]{3,2,1,0:T(8,128)(2,1)}, u32[]{:S(2)}, u32[]{:S(2)}) %collective-permute-start.4) | collective-permute-done | bytes 1048608 | tf_op jit(solution)/shard_map/ppermute | solution.py:389
  79.7 1.7 collective-permute-start.8
  81.4 1.1 slice.88
  82.5 1.1 slice.85
  83.6 1.6 collective-permute-start.9
  85.2 0.5 collective-permute-start.6
  85.7 0.5 collective-permute-done.2.refs_5_
  86.2 0.5 collective-permute-start.15
  86.7 10.7 %collective-permute-done.8.refs_11_ = bf16[2,4,64,512]{3,2,1,0:T(8,128)(2,1)S(1)} collective-permute-done((bf16[2,4,64,512]{3,2,1,0:T(8,128)(2,1)S(1)}, bf16[2,4,64,512]{3,2,1,0:T(8,128)(2,1)S(1)}, u32[]{:S(2)}, u32[]{:S(2)}) %collective-permute-start.8) | collective-permute-done | bytes 524320 | tf_op jit(solution)/shard_map/ppermute | solution.py:389
  97.5 0.7 collective-permute-start.7
  98.3 10.0 %collective-permute-done.6.refs_9_ = bf16[2,4,64,512]{3,2,1,0:T(8,128)(2,1)S(1)} collective-permute-done((bf16[2,4,64,512]{3,2,1,0:T(8,128)(2,1)S(1)}, bf16[2,4,64,512]{3,2,1,0:T(8,128)(2,1)S(1)}, u32[]{:S(2)}, u32[]{:S(2)}) %collective-permute-start.6) | collective-permute-done | bytes 524320 | tf_op jit(solution)/shard_map/ppermute | solution.py:389
  108.2 3.7 %collective-permute-done.7.refs_10_ = bf16[2,4,64,512]{3,2,1,0:T(8,128)(2,1)S(1)} collective-permute-done((bf16[2,4,64,512]{3,2,1,0:T(8,128)(2,1)S(1)}, bf16[2,4,64,512]{3,2,1,0:T(8,128)(2,1)S(1)}, u32[]{:S(2)}, u32[]{:S(2)}) %collective-permute-start.7) | collective-permute-done | bytes 524320 | tf_op jit(solution)/shard_map/ppermute | solution.py:389
  111.9 0.5 collective-permute-start.19
  112.4 0.1 collective-permute-start.16
  112.5 0.5 collective-permute-start.17
  113.0 0.8 collective-permute-done.18.refs_21_
  113.8 0.7 collective-permute-done.19.refs_22_
  114.6 0.7 collective-permute-done.16.refs_19_
  115.3 0.7 collective-permute-done.17.refs_20_
  116.1 0.8 copy-done.24
  116.9 71.8 %shard_map.92 = bf16[256,2,16,128]{3,2,1,0:T(8,128)(2,1)} custom-call(s32[8]{0:T(128)} %copy-done.9, s32[256]{0:T(256)} %get-tuple-element.36.pos_ref, bf16[128,2,16,128]{3,2,1,0:T(8,128)(2,1)} %get-tuple-element.69.refs_0_, bf16[128,2,16,128]{3,2,1,0:T(8,128)(2,1)} %copy-done.10, bf16[2,128,64,512]{3,2,1,0:T(8,128)(2,1)} %refs_2_.1, ...), custom_call_target="tpu_custom_call" | custom-call | flops 25769803776 | bytes 111149056 | tf_op jit(solution)/shard_map/pallas_call | solution.py:314
  188.7 54.6 %all_to_all.15.weighted_ref = bf16[32,2,4,2,16,128]{5,4,3,2,1,0:T(8,128)(2,1)S(1)} all-to-all(bf16[32,2,4,2,16,128]{5,4,3,2,1,0:T(8,128)(2,1)} %bitcast.68), channel_id=1, replica_groups=mesh['mom'=2,'pts'=16] {'mom','pts'}, dimensions={0} | all-to-all | bytes 4194304 | tf_op jit(solution)/shard_map/all_to_all | solution.py:495
  243.3 51.4 %all_to_all.16 = bf16[32,4,2,32,128]{4,3,2,1,0:T(8,128)(2,1)S(1)} all-to-all(bf16[32,4,2,32,128]{4,3,2,1,0:T(8,128)(2,1)S(1)} %bitcast.67), channel_id=1, replica_groups=mesh['mom'=2,'pts'=16] {'mom','pts'}, dimensions={0} | all-to-all | bytes 4194304 | tf_op jit(solution)/shard_map/all_to_all | solution.py:478
  294.7 1.8 shard_map.93
  296.5 0.8 pad_maximum_fusion
  297.3 2.8 all-to-all-start.2
  300.2 0.1 copy.15
  300.3 1.4 dynamic-slice_convert_fusion
  301.8 14.0 %all-to-all-done.2 = bf16[32,4,2,8,128]{4,3,2,1,0:T(8,128)(2,1)S(1)} async-done(((bf16[32,4,2,8,128]{4,3,2,1,0:T(8,128)(2,1)}), bf16[32,4,2,8,128]{4,3,2,1,0:T(8,128)(2,1)S(1)}, u32[]{:S(2)}, u32[]{:S(2)}) %all-to-all-start.2) | async-done | bytes 524320 | tf_op jit(solution)/shard_map/all_to_all | solution.py:498
  315.8 1.0 gather_fusion.1
  316.9 0.1 convert_element_type.31
  317.0 0.2 fusion.29
  317.3 0.1 select_bitcast_fusion
  317.4 0.1 fusion
  317.5 0.5 copy-done.5
  318.1 0.2 fusion.4
  318.3 0.3 fusion.13
  318.6 0.1 maximum_bitcast_fusion.1
  318.8 0.1 maximum_bitcast_fusion.2
  318.9 1.2 maximum_bitcast_fusion
  (77 shorter events, 0.3 us)
Async XLA Ops:
  0.0 5.8 %copy-start.26 = (s32[8]{0:T(128)S(1)}, s32[8]{0:T(128)}, u32[]{:S(2)}) copy-start(s32[8]{0:T(128)} %constant.114.clone) | copy-start | bytes 100
  2.8 29.4 %collective-permute-start = (bf16[2,8,64,512]{3,2,1,0:T(8,128)(2,1)}, bf16[2,8,64,512]{3,2,1,0:T(8,128)(2,1)}, u32[]{:S(2)}, u32[]{:S(2)}) collective-permute-start(bf16[2,8,64,512]{3,2,1,0:T(8,128)(2,1)} %get-tuple-element.68), channel_id=1, source_target_pairs={{0,16},{16,0},{1,17},{17,1},{2,18},{18,2},{3,19},{19,3},{4,20},{20... | collective-permute-start | bytes 3145736 | tf_op jit(solution)/shard_map/ppermute | solution.py:385
  5.7 45.9 %collective-permute-start.1 = (bf16[2,8,64,512]{3,2,1,0:T(8,128)(2,1)S(1)}, bf16[2,8,64,512]{3,2,1,0:T(8,128)(2,1)}, u32[]{:S(2)}, u32[]{:S(2)}) collective-permute-start(bf16[2,8,64,512]{3,2,1,0:T(8,128)(2,1)S(1)} %get-tuple-element.67), channel_id=1, source_target_pairs={{0,16},{16,0},{1,17},{17,1},{2,18},{18,2},{3,19},{19,3},{4,20},{20... | collective-permute-start | bytes 3145736 | tf_op jit(solution)/shard_map/ppermute | solution.py:385
  5.8 11.7 %copy-start.9 = (s32[8]{0:T(128)}, s32[8]{0:T(128)S(1)}, u32[]{:S(2)}) copy-start(s32[8]{0:T(128)S(1)} %xor_multiply_fusion.base_ref) | copy-start | bytes 100
  5.9 11.6 %copy-start.1 = (bf16[2,128,32,128]{3,2,1,0:T(8,128)(2,1)S(1)}, bf16[2,128,32,128]{3,2,1,0:T(8,128)(2,1)}, u32[]{:S(2)}) copy-start(bf16[2,128,32,128]{3,2,1,0:T(8,128)(2,1)} %cond_ref.1) | copy-start | bytes 6291460
  17.5 3.4 %copy-start = (bf16[2,2,1,128,64,128]{5,4,3,2,1,0:T(8,128)(2,1)S(1)}, bf16[2,2,1,128,64,128]{5,4,3,2,1,0:T(8,128)(2,1)}, u32[]{:S(2)}) copy-start(bf16[2,2,1,128,64,128]{5,4,3,2,1,0:T(8,128)(2,1)} %amp_ref.1) | copy-start | bytes 25165828
  20.9 8.6 %copy-start.7 = (s32[256]{0:T(256)S(1)}, s32[256]{0:T(256)}, u32[]{:S(2)}) copy-start(s32[256]{0:T(256)} %param.15) | copy-start | bytes 3076
  32.2 27.7 %collective-permute-start.5 = (bf16[2,8,64,512]{3,2,1,0:T(8,128)(2,1)}, bf16[2,8,64,512]{3,2,1,0:T(8,128)(2,1)}, u32[]{:S(2)}, u32[]{:S(2)}) collective-permute-start(bf16[2,8,64,512]{3,2,1,0:T(8,128)(2,1)} %collective-permute-done.refs_4_), channel_id=1, source_target_pairs={{0,4},{1,5},{2,6},{3,7},{4,0},{5,1},{6,2},{7,3},{8,12},{9,13},{10,... | collective-permute-start | bytes 3145736 | tf_op jit(solution)/shard_map/ppermute | solution.py:389
  34.3 27.2 %collective-permute-start.3 = (bf16[2,8,64,512]{3,2,1,0:T(8,128)(2,1)}, bf16[2,8,64,512]{3,2,1,0:T(8,128)(2,1)}, u32[]{:S(2)}, u32[]{:S(2)}) collective-permute-start(bf16[2,8,64,512]{3,2,1,0:T(8,128)(2,1)} %collective-permute-done.refs_4_), channel_id=1, source_target_pairs={{0,2},{1,3},{2,0},{3,1},{4,6},{5,7},{6,4},{7,5},{8,10},{9,11},{10,... | collective-permute-start | bytes 3145736 | tf_op jit(solution)/shard_map/ppermute | solution.py:389
  51.7 28.0 %collective-permute-start.4 = (bf16[2,8,64,512]{3,2,1,0:T(8,128)(2,1)}, bf16[2,8,64,512]{3,2,1,0:T(8,128)(2,1)}, u32[]{:S(2)}, u32[]{:S(2)}) collective-permute-start(bf16[2,8,64,512]{3,2,1,0:T(8,128)(2,1)} %collective-permute-done.1.refs_3_), channel_id=1, source_target_pairs={{0,4},{1,5},{2,6},{3,7},{4,0},{5,1},{6,2},{7,3},{8,12},{9,13},{10,... | collective-permute-start | bytes 3145736 | tf_op jit(solution)/shard_map/ppermute | solution.py:389
  53.5 2.1 copy-start.4
  55.7 2.8 copy-start.3
  58.5 25.1 %collective-permute-start.20 = (bf16[128,2,16,128]{3,2,1,0:T(8,128)(2,1)S(1)}, bf16[128,2,16,128]{3,2,1,0:T(8,128)(2,1)S(1)}, u32[]{:S(2)}, u32[]{:S(2)}) collective-permute-start(bf16[128,2,16,128]{3,2,1,0:T(8,128)(2,1)S(1)} %copy-done.3), channel_id=1, source_target_pairs={{0,16},{16,0},{1,17},{17,1},{2,18},{18,2},{3,19},{19,3},{4,20},{20... | collective-permute-start | bytes 3145736 | tf_op jit(solution)/shard_map/ppermute | solution.py:385
  60.0 25.2 %collective-permute-start.11 = (bf16[2,8,64,512]{3,2,1,0:T(8,128)(2,1)}, bf16[2,8,64,512]{3,2,1,0:T(8,128)(2,1)S(1)}, u32[]{:S(2)}, u32[]{:S(2)}) collective-permute-start(bf16[2,8,64,512]{3,2,1,0:T(8,128)(2,1)} %collective-permute-done.refs_4_), channel_id=1, source_target_pairs={{0,1},{1,0},{2,3},{3,2},{4,5},{5,4},{6,7},{7,6},{8,9},{9,8},{10,11... | collective-permute-start | bytes 3145736 | tf_op jit(solution)/shard_map/ppermute | solution.py:389
  60.0 26.2 %collective-permute-start.2 = (bf16[2,8,64,512]{3,2,1,0:T(8,128)(2,1)}, bf16[2,8,64,512]{3,2,1,0:T(8,128)(2,1)S(1)}, u32[]{:S(2)}, u32[]{:S(2)}) collective-permute-start(bf16[2,8,64,512]{3,2,1,0:T(8,128)(2,1)} %collective-permute-done.1.refs_3_), channel_id=1, source_target_pairs={{0,2},{1,3},{2,0},{3,1},{4,6},{5,7},{6,4},{7,5},{8,10},{9,11},{10,... | collective-permute-start | bytes 3145736 | tf_op jit(solution)/shard_map/ppermute | solution.py:389
  61.5 24.7 %collective-permute-start.10 = (bf16[2,8,64,512]{3,2,1,0:T(8,128)(2,1)}, bf16[2,8,64,512]{3,2,1,0:T(8,128)(2,1)S(1)}, u32[]{:S(2)}, u32[]{:S(2)}) collective-permute-start(bf16[2,8,64,512]{3,2,1,0:T(8,128)(2,1)} %collective-permute-done.1.refs_3_), channel_id=1, source_target_pairs={{0,1},{1,0},{2,3},{3,2},{4,5},{5,4},{6,7},{7,6},{8,9},{9,8},{10,11... | collective-permute-start | bytes 3145736 | tf_op jit(solution)/shard_map/ppermute | solution.py:389
  79.7 17.8 %collective-permute-start.8 = (bf16[2,4,64,512]{3,2,1,0:T(8,128)(2,1)S(1)}, bf16[2,4,64,512]{3,2,1,0:T(8,128)(2,1)S(1)}, u32[]{:S(2)}, u32[]{:S(2)}) collective-permute-start(bf16[2,4,64,512]{3,2,1,0:T(8,128)(2,1)S(1)} %slice.87), channel_id=1, source_target_pairs={{0,2},{1,3},{2,0},{3,1},{4,6},{5,7},{6,4},{7,5},{8,10},{9,11},{10,... | collective-permute-start | bytes 1572872 | tf_op jit(solution)/shard_map/ppermute | solution.py:389
  83.5 29.0 %copy-start.10 = (bf16[128,2,16,128]{3,2,1,0:T(8,128)(2,1)}, bf16[128,2,16,128]{3,2,1,0:T(8,128)(2,1)S(1)}, u32[]{:S(2)}) copy-start(bf16[128,2,16,128]{3,2,1,0:T(8,128)(2,1)S(1)} %collective-permute-done.20.refs_1_) | copy-start | bytes 3145732
  83.6 13.9 %collective-permute-start.9 = (bf16[2,4,64,512]{3,2,1,0:T(8,128)(2,1)S(1)}, bf16[2,4,64,512]{3,2,1,0:T(8,128)(2,1)S(1)}, u32[]{:S(2)}, u32[]{:S(2)}) collective-permute-start(bf16[2,4,64,512]{3,2,1,0:T(8,128)(2,1)S(1)} %slice.88), channel_id=1, source_target_pairs={{0,4},{1,5},{2,6},{3,7},{4,0},{5,1},{6,2},{7,3},{8,12},{9,13},{10,... | collective-permute-start | bytes 1572872 | tf_op jit(solution)/shard_map/ppermute | solution.py:389
  85.2 27.8 %copy-start.11 = (bf16[2,8,64,512]{3,2,1,0:T(8,128)(2,1)}, bf16[2,8,64,512]{3,2,1,0:T(8,128)(2,1)S(1)}, u32[]{:S(2)}) copy-start(bf16[2,8,64,512]{3,2,1,0:T(8,128)(2,1)S(1)} %collective-permute-done.11.refs_14_) | copy-start | bytes 3145732
  85.2 23.0 %collective-permute-start.6 = (bf16[2,4,64,512]{3,2,1,0:T(8,128)(2,1)S(1)}, bf16[2,4,64,512]{3,2,1,0:T(8,128)(2,1)S(1)}, u32[]{:S(2)}, u32[]{:S(2)}) collective-permute-start(bf16[2,4,64,512]{3,2,1,0:T(8,128)(2,1)S(1)} %slice.85), channel_id=1, source_target_pairs={{0,2},{1,3},{2,0},{3,1},{4,6},{5,7},{6,4},{7,5},{8,10},{9,11},{10,... | collective-permute-start | bytes 1572872 | tf_op jit(solution)/shard_map/ppermute | solution.py:389
  86.2 30.7 %copy-start.6 = (bf16[2,8,64,512]{3,2,1,0:T(8,128)(2,1)}, bf16[2,8,64,512]{3,2,1,0:T(8,128)(2,1)S(1)}, u32[]{:S(2)}) copy-start(bf16[2,8,64,512]{3,2,1,0:T(8,128)(2,1)S(1)} %collective-permute-done.2.refs_5_) | copy-start | bytes 3145732
  86.2 25.7 %collective-permute-start.13 = (bf16[2,8,64,512]{3,2,1,0:T(8,128)(2,1)}, bf16[2,8,64,512]{3,2,1,0:T(8,128)(2,1)S(1)}, u32[]{:S(2)}, u32[]{:S(2)}) collective-permute-start(bf16[2,8,64,512]{3,2,1,0:T(8,128)(2,1)} %collective-permute-done.3.refs_6_), channel_id=1, source_target_pairs={{0,1},{1,0},{2,3},{3,2},{4,5},{5,4},{6,7},{7,6},{8,9},{9,8},{10,11... | collective-permute-start | bytes 3145736 | tf_op jit(solution)/shard_map/ppermute | solution.py:389
  86.2 26.8 %copy-start.12 = (bf16[2,8,64,512]{3,2,1,0:T(8,128)(2,1)}, bf16[2,8,64,512]{3,2,1,0:T(8,128)(2,1)S(1)}, u32[]{:S(2)}) copy-start(bf16[2,8,64,512]{3,2,1,0:T(8,128)(2,1)S(1)} %collective-permute-done.10.refs_13_) | copy-start | bytes 3145732
  86.2 26.2 %collective-permute-start.15 = (bf16[2,8,64,512]{3,2,1,0:T(8,128)(2,1)}, bf16[2,8,64,512]{3,2,1,0:T(8,128)(2,1)S(1)}, u32[]{:S(2)}, u32[]{:S(2)}) collective-permute-start(bf16[2,8,64,512]{3,2,1,0:T(8,128)(2,1)} %collective-permute-done.5.refs_8_), channel_id=1, source_target_pairs={{0,1},{1,0},{2,3},{3,2},{4,5},{5,4},{6,7},{7,6},{8,9},{9,8},{10,11... | collective-permute-start | bytes 3145736 | tf_op jit(solution)/shard_map/ppermute | solution.py:389
  97.4 19.5 %copy-start.17 = (bf16[2,4,64,512]{3,2,1,0:T(8,128)(2,1)}, bf16[2,4,64,512]{3,2,1,0:T(8,128)(2,1)S(1)}, u32[]{:S(2)}) copy-start(bf16[2,4,64,512]{3,2,1,0:T(8,128)(2,1)S(1)} %collective-permute-done.8.refs_11_) | copy-start | bytes 1572868
  97.4 15.1 %collective-permute-start.12 = (bf16[2,8,64,512]{3,2,1,0:T(8,128)(2,1)S(1)}, bf16[2,8,64,512]{3,2,1,0:T(8,128)(2,1)S(1)}, u32[]{:S(2)}, u32[]{:S(2)}) collective-permute-start(bf16[2,8,64,512]{3,2,1,0:T(8,128)(2,1)S(1)} %collective-permute-done.2.refs_5_), channel_id=1, source_target_pairs={{0,1},{1,0},{2,3},{3,2},{4,5},{5,4},{6,7},{7,6},{8,9},{9,8},{10,11... | collective-permute-start | bytes 3145736 | tf_op jit(solution)/shard_map/ppermute | solution.py:389
  97.5 18.6 %copy-start.18 = (bf16[2,4,64,512]{3,2,1,0:T(8,128)(2,1)}, bf16[2,4,64,512]{3,2,1,0:T(8,128)(2,1)S(1)}, u32[]{:S(2)}) copy-start(bf16[2,4,64,512]{3,2,1,0:T(8,128)(2,1)S(1)} %collective-permute-done.9.refs_12_) | copy-start | bytes 1572868
  97.5 14.4 %collective-permute-start.7 = (bf16[2,4,64,512]{3,2,1,0:T(8,128)(2,1)S(1)}, bf16[2,4,64,512]{3,2,1,0:T(8,128)(2,1)S(1)}, u32[]{:S(2)}, u32[]{:S(2)}) collective-permute-start(bf16[2,4,64,512]{3,2,1,0:T(8,128)(2,1)S(1)} %slice.86), channel_id=1, source_target_pairs={{0,4},{1,5},{2,6},{3,7},{4,0},{5,1},{6,2},{7,3},{8,12},{9,13},{10,... | collective-permute-start | bytes 1572872 | tf_op jit(solution)/shard_map/ppermute | solution.py:389
  108.2 7.9 %copy-start.19 = (bf16[2,4,64,512]{3,2,1,0:T(8,128)(2,1)}, bf16[2,4,64,512]{3,2,1,0:T(8,128)(2,1)S(1)}, u32[]{:S(2)}) copy-start(bf16[2,4,64,512]{3,2,1,0:T(8,128)(2,1)S(1)} %collective-permute-done.6.refs_9_) | copy-start | bytes 1572868
  108.2 4.8 %collective-permute-start.14 = (bf16[2,8,64,512]{3,2,1,0:T(8,128)(2,1)}, bf16[2,8,64,512]{3,2,1,0:T(8,128)(2,1)S(1)}, u32[]{:S(2)}, u32[]{:S(2)}) collective-permute-start(bf16[2,8,64,512]{3,2,1,0:T(8,128)(2,1)} %collective-permute-done.4.refs_7_), channel_id=1, source_target_pairs={{0,1},{1,0},{2,3},{3,2},{4,5},{5,4},{6,7},{7,6},{8,9},{9,8},{10,11... | collective-permute-start | bytes 3145736 | tf_op jit(solution)/shard_map/ppermute | solution.py:389
  111.9 4.2 %copy-start.20 = (bf16[2,4,64,512]{3,2,1,0:T(8,128)(2,1)}, bf16[2,4,64,512]{3,2,1,0:T(8,128)(2,1)S(1)}, u32[]{:S(2)}) copy-start(bf16[2,4,64,512]{3,2,1,0:T(8,128)(2,1)S(1)} %collective-permute-done.7.refs_10_) | copy-start | bytes 1572868
  111.9 1.9 collective-permute-start.18
  111.9 1.9 copy-start.13
  111.9 2.6 collective-permute-start.19
  112.4 2.1 copy-start.14
  112.4 2.9 collective-permute-start.16
  112.5 2.8 copy-start.15
  112.5 3.5 %collective-permute-start.17 = (bf16[2,4,64,512]{3,2,1,0:T(8,128)(2,1)S(1)}, bf16[2,4,64,512]{3,2,1,0:T(8,128)(2,1)S(1)}, u32[]{:S(2)}, u32[]{:S(2)}) collective-permute-start(bf16[2,4,64,512]{3,2,1,0:T(8,128)(2,1)S(1)} %collective-permute-done.7.refs_10_), channel_id=1, source_target_pairs={{0,1},{1,0},{2,3},{3,2},{4,5},{5,4},{6,7},{7,6},{8,9},{9,8},{10,11... | collective-permute-start | bytes 1572872 | tf_op jit(solution)/shard_map/ppermute | solution.py:389
  113.0 3.1 copy-start.16
  113.8 2.3 copy-start.21
  114.6 1.5 copy-start.22
  115.3 0.8 copy-start.23
  116.1 0.8 copy-start.24
  188.7 54.6 %copy-start.2 = (bf16[128,2,32,128]{3,2,1,0:T(8,128)(2,1)S(1)}, bf16[128,2,32,128]{3,2,1,0:T(8,128)(2,1)}, u32[]{:S(2)}) copy-start(bf16[128,2,32,128]{3,2,1,0:T(8,128)(2,1)} %gather_fusion) | copy-start | bytes 6291460
  294.7 5.5 %copy-start.8 = (f32[128,4]{0,1:T(4,128)S(1)}, f32[128,4]{0,1:T(4,128)}, u32[]{:S(2)}) copy-start(f32[128,4]{0,1:T(4,128)} %param.13) | copy-start | bytes 6148
  294.7 5.6 %copy-start.25 = (s32[128]{0:T(128)S(1)}, s32[128]{0:T(128)}, u32[]{:S(2)}) copy-start(s32[128]{0:T(128)} %param.16) | copy-start | bytes 1540
  297.3 18.5 %all-to-all-start.2 = ((bf16[32,4,2,8,128]{4,3,2,1,0:T(8,128)(2,1)}), bf16[32,4,2,8,128]{4,3,2,1,0:T(8,128)(2,1)S(1)}, u32[]{:S(2)}, u32[]{:S(2)}) async-start(bf16[32,4,2,8,128]{4,3,2,1,0:T(8,128)(2,1)} %pad_maximum_fusion), calls=%async_computation.2 | async-start | bytes 1048576 | tf_op jit(solution)/shard_map/all_to_all | solution.py:498
  317.2 0.8 copy-start.5

commit v4 on v3

--- a/solution.py
+++ b/solution.py
@@ -155,19 +155,12 @@
 
 
 def main_body(layout, base_ref, pos_ref, *refs):
-    own_blocks, block, sizes, points, first, last = layout
+    own_blocks, block, sizes, points = layout
     half_own, half_other, own_ref = refs[:3]
     count = sum(len(group) for group in sizes)
-    flat = list(refs[3 : 3 + count])
-    groups = []
-    for group in sizes:
-        groups.append([flat.pop(0) for _ in group])
-    rest = list(refs[3 + count :])
-    screen_ref, forward_ref, backward_ref = rest[:3]
-    rest = rest[3:]
-    before_ref = None if first else rest.pop(0)
-    out_ref, pair_ref = rest
-    blocks = own_blocks + len(groups)
+    pieces = refs[3 : 3 + count]
+    screen_ref, forward_ref, backward_ref, out_ref, pair_ref, held_ref, sems = refs[3 + count :]
+    blocks = own_blocks + len(sizes)
     total = blocks * block
     rows = 4 * points
     pitch = rows + 1
@@ -177,51 +170,69 @@
     into = half_signs(1.0, -1.0)
     back = half_signs(-1.0, 1.0)
 
-    def make_pairs(source, half_ref, half_start, start, size):
-        for kk in range(size):
+    def make_pairs(source, half_ref, half_start, start, offset):
+        for kk in range(block):
             half = half_ref[half_start + kk].reshape(2 * points, 128)
             turned = (pltpu.roll(half.astype(F32), 64, 1) * into).astype(BF16)
             stacked = jnp.concatenate([half, turned], axis=0)
-            val = source[:, kk].reshape(128, width)
+            val = source[:, offset + kk].reshape(128, width)
             pairs = jnp.dot(stacked, val, preferred_element_type=F32)
             at = (start + kk) * pitch
             for l in range(lanes):
                 pair_ref[l, pl.ds(at, rows), :] = pairs[:, l * 128 : (l + 1) * 128]
 
-    def make_weighted(source, half_ref, half_start, start, size):
-        for kk in range(size):
+    def make_weighted(source, half_ref, half_start, start, offset):
+        for kk in range(block):
             k = start + kk
             at = k * pitch
             field = jnp.concatenate(
                 [pair_ref[l, pl.ds(at, rows), :] for l in range(lanes)], axis=1
             ).astype(BF16)
-            val = source[:, kk].reshape(128, width)
+            val = source[:, offset + kk].reshape(128, width)
             both = lax.dot_general(
                 field, val, (((1,), (1,)), ((), ())), preferred_element_type=F32
             )
             half = rows // 2
             weighted = both[:half] + pltpu.roll(both[half:], 64, 1) * back
-            if not first:
-                weighted = before_ref[k] + weighted
-            if last:
-                out_ref[pos_ref[k]] = weighted.astype(BF16).reshape(2, points, 128)
-            else:
-                out_ref[k] = weighted
+            out_ref[pos_ref[k]] = weighted.astype(BF16).reshape(2, points, 128)
 
     def each_block(work, index):
         @pl.when(index < own_blocks)
         def _():
-            work(own_ref, half_own, index * block, index * block, block)
-
-        for t, (group, extents) in enumerate(zip(groups, sizes)):
-
-            @pl.when(index == own_blocks + t)
-            def _():
-                done = 0
-                for ref, extent in zip(group, extents):
-                    start = (own_blocks + t) * block + done
-                    work(ref, half_other, base_ref[t] + done, start, extent)
-                    done += extent
+            work(own_ref, half_own, index * block, index * block, 0)
+
+        @pl.when(index >= own_blocks)
+        def _():
+            t = index - own_blocks
+            work(held_ref, half_other, base_ref[t], index * block, t * block)
+
+    copies = []
+    number = 0
+    for t, extents in enumerate(sizes):
+        start = t * block
+        copies.append([])
+        for extent in extents:
+            copies[-1].append(
+                pltpu.make_async_copy(
+                    pieces[number], held_ref.at[:, pl.ds(start, extent)], sems.at[number]
+                )
+            )
+            start += extent
+            number += 1
+
+    for t, group in enumerate(copies):
+
+        @pl.when(step == min(t, own_blocks - 1))
+        def _():
+            for copy in group:
+                copy.start()
+
+    for t, group in enumerate(copies):
+
+        @pl.when(step == own_blocks + t)
+        def _():
+            for copy in group:
+                copy.wait()
 
     @pl.when(step < blocks)
     def _():
@@ -265,7 +276,7 @@
         each_block(make_weighted, step - blocks - points)
 
 
-def main_call(half_own, half_other, own, chunk, pieces, screen, tables, base, pos, before, last):
+def main_call(half_own, half_other, own, pieces, screen, tables, base, pos):
     slots, _, points, _ = half_own.shape
     bands = own.shape[2]
     block = sum(piece.shape[1] for piece in pieces[0])
@@ -273,14 +284,13 @@
     own_blocks = slots // block
     blocks = own_blocks + len(pieces)
     total = blocks * block
-    first = before is None
     sizes = tuple(tuple(piece.shape[1] for piece in group) for group in pieces)
     flat = [piece for group in pieces for piece in group]
 
     def own_map(s, *_):
         early = jnp.minimum(s, own_blocks - 1)
         late = jnp.clip(s - blocks - points, 0, own_blocks - 1)
-        return (0, jnp.where(s < blocks, early, late), 0, chunk)
+        return (0, jnp.where(s < blocks, early, late), 0, 0)
 
     def whole(shape):
         return pl.BlockSpec(
@@ -292,34 +302,32 @@
         whole(half_other.shape),
         pl.BlockSpec((2, block, bands, width), own_map),
     ]
-    in_specs += [whole(piece.shape) for piece in flat]
+    in_specs += [pl.BlockSpec(memory_space=pl.ANY) for _ in flat]
     in_specs += [
         pl.BlockSpec(
-            (1, 2, total, width), lambda s, *_: (jnp.clip(s - blocks, 0, points - 1), 0, 0, chunk)
+            (1, 2, total, width), lambda s, *_: (jnp.clip(s - blocks, 0, points - 1), 0, 0, 0)
         ),
         whole(tables[0].shape),
         whole(tables[1].shape),
     ]
     operands = [half_own, half_other, own, *flat, screen, *tables]
-    if not first:
-        in_specs.append(whole(before.shape))
-        operands.append(before)
-    if last:
-        out = jax.ShapeDtypeStruct((total, 2, points, 128), BF16)
-    else:
-        out = jax.ShapeDtypeStruct((total, 2 * points, 128), F32)
+    out = jax.ShapeDtypeStruct((total, 2, points, 128), BF16)
     columns = 2 * points * width
     work = 8 * columns * total * total * 2 + 4 * columns * total * 2 * bands * 4
     traffic = 2 * total * (2 * bands * width * 3 + points * (2 * width + 4 * bands))
     return pl.pallas_call(
-        functools.partial(main_body, (own_blocks, block, sizes, points, first, last)),
+        functools.partial(main_body, (own_blocks, block, sizes, points)),
         out_shape=out,
         grid_spec=pltpu.PrefetchScalarGridSpec(
             num_scalar_prefetch=2,
             grid=(2 * blocks + points,),
             in_specs=in_specs,
             out_specs=whole(out.shape),
-            scratch_shapes=[pltpu.VMEM((width // 128, total * (4 * points + 1), 128), F32)],
+            scratch_shapes=[
+                pltpu.VMEM((width // 128, total * (4 * points + 1), 128), F32),
+                pltpu.VMEM((2, len(pieces) * block, bands, width), BF16),
+                pltpu.SemaphoreType.DMA((len(flat),)),
+            ],
         ),
         compiler_params=pltpu.CompilerParams(vmem_limit_bytes=62 * MIB),
         cost_estimate=pl.CostEstimate(
@@ -428,9 +436,7 @@
     where = (jnp.arange(groups, dtype=jnp.int32) - mom) % groups
     halves = half_call(amplitudes, cond_orbitals, where, groups)
     screen = jnp.transpose(screened, (2, 0, 1, 3))
-    fetched[-1], half_sent, screen = lax.optimization_barrier(
-        (fetched[-1], halves[1], screen)
-    )
+    fetched[-1], half_sent = lax.optimization_barrier((fetched[-1], halves[1]))
     streams = [with_cores(gather_chips(here)) for here in fetched]
     pieces = [sum(groups_of, []) for groups_of in zip(*streams)]
 
@@ -468,8 +474,8 @@
     )
     cond_send = jnp.take(jnp.swapaxes(cond_orbitals, 0, 1), paired, axis=0, mode="clip")
     cond_send = cond_send.reshape((devices, pairs) + cond_send.shape[1:])
-    half_sent, forward, backward, place_here, cond_send = lax.optimization_barrier(
-        (half_sent, forward, backward, place_here, cond_send)
+    half_sent, forward, backward, place_here, cond_send, screen = lax.optimization_barrier(
+        (half_sent, forward, backward, place_here, cond_send, screen)
     )
     half_other = swap_mom(half_sent)
     cond_send, pieces, half_other = lax.optimization_barrier(
@@ -482,14 +488,11 @@
         halves[0],
         half_other,
         val_orbitals,
-        0,
         pieces,
         screen,
         (forward, backward),
         order * eighth,
         place_here,
-        None,
-        True,
     )
     send = weighted.reshape((devices, 2, pairs) + weighted.shape[1:])
     weighted = lax.all_to_all(send, ("mom", "pts"), 0, 0, tiled=True)

time: 321 us -> 326 us (1.016)
  waiting for transfers between devices: 71.9 us -> 84.2 us
  Pallas kernels: 82.2 us -> 77 us
    ppermute x3, waiting for transfers between devices: 13 us -> 38.2 us  [swap_mom(): return lax.ppermute(value, 'mom', [(0, 1), (1, 0)])]
    ppermute x18, waiting for transfers between devices: 44.8 us -> 31.8 us  [swap_pts(): lax.ppermute(value, 'pts', [(i, i ^ mask) for i in range(lax.axis_size('p...]
    pallas_call x1, Pallas kernels: 71.8 us -> 66.6 us  [main_call(): pl.pallas_call(functools.partial(main_body, (own_blocks, block, sizes, po...]
  transfers between devices with their start and end apart: 22 -> 22, of which waited for: 11 -> 13; matrix products, arithmetic and copies ran while one was open for 8% -> 8% of each run, Pallas kernels for 3% -> 3%
where the time goes in v4:
time: 326 us; the launch traced here: 325 us
  blocking collectives  105 us (32%)
  waiting for transfers between devices  84.2 us (26%)
  Pallas kernels  77 us (24%)
  local copies, waits for them, and re-layouts  27.7 us (8%)
  starting transfers between devices  19.8 us (6%)
  other arithmetic  11.4 us (3%)
    pallas_call x1, Pallas kernels, main_call(): pl.pallas_call(functools.partial(main_body, (own_blocks, block, sizes, po...  66.6 us
    all_to_all x1, blocking collectives, fast_path(): weighted = lax.all_to_all(send, ('mom', 'pts'), 0, 0, tiled=True)  53.5 us
    all_to_all x1, blocking collectives, fast_path(): cond_pairs = lax.all_to_all(cond_send, ('mom', 'pts'), 0, 0, tiled=True)  51.4 us
    ppermute x3, waiting for transfers between devices, swap_mom(): return lax.ppermute(value, 'mom', [(0, 1), (1, 0)])  38.2 us
    ppermute x18, waiting for transfers between devices, swap_pts(): lax.ppermute(value, 'pts', [(i, i ^ mask) for i in range(lax.axis_size('p...  31.8 us
    unnamed x56, local copies, waits for them, and re-layouts  16.4 us
    all_to_all x1, waiting for transfers between devices, fast_path(): back = lax.all_to_all(combined, ('mom', 'pts'), 0, 0, tiled=True)  14.3 us
    ppermute x18, starting transfers between devices, swap_pts(): lax.ppermute(value, 'pts', [(i, i ^ mask) for i in range(lax.axis_size('p...  12.8 us
  transfers between devices with their start and end apart: 22, of which 13 were waited for; matrix products, arithmetic and copies ran while one was open for 8% of the time, Pallas kernels for 3%

profile of v4, /device:TPU:0, one launch (start us, length us, event | category | flops | bytes accessed | tf_op | source)
XLA Modules:
  0.0 325.4 jit_solution(13755798239253314894)
XLA Ops:
  0.0 2.9 constant_dynamic-slice_fusion.1
  2.9 3.0 collective-permute-start
  6.0 0.1 add.115
  6.1 3.4 %copy-done = bf16[2,2,1,128,64,128]{5,4,3,2,1,0:T(8,128)(2,1)S(1)} copy-done((bf16[2,2,1,128,64,128]{5,4,3,2,1,0:T(8,128)(2,1)S(1)}, bf16[2,2,1,128,64,128]{5,4,3,2,1,0:T(8,128)(2,1)}, u32[]{:S(2)}) %copy-start) | copy-done | bytes 8388632
  9.5 8.6 %shard_map.91 = bf16[2,128,2,16,128]{4,3,2,1,0:T(8,128)(2,1)S(1)} custom-call(s32[2]{0:T(128)S(1)} %and_select_fusion.3.where_ref, bf16[2,2,1,128,64,128]{5,4,3,2,1,0:T(8,128)(2,1)S(1)} %copy-done, bf16[2,128,32,128]{3,2,1,0:T(8,128)(2,1)S(1)} %copy-done.1), custom_call_target="tpu_custom_call" | custom-call | tf_op jit(solution)/shard_map/pallas_call | solution.py:139
  18.1 0.2 select_reduce_fusion.1
  18.4 0.8 select_reduce_fusion
  19.1 1.7 slice_bitcast_fusion
  20.8 9.4 %collective-permute-done.refs_4_ = bf16[2,8,64,512]{3,2,1,0:T(8,128)(2,1)} collective-permute-done((bf16[2,8,64,512]{3,2,1,0:T(8,128)(2,1)}, bf16[2,8,64,512]{3,2,1,0:T(8,128)(2,1)}, u32[]{:S(2)}, u32[]{:S(2)}) %collective-permute-start) | collective-permute-done | bytes 1048608 | tf_op jit(solution)/shard_map/ppermute | solution.py:393
  30.2 2.1 collective-permute-start.5
  32.3 1.5 collective-permute-start.3
  33.8 2.9 fusion.23
  36.7 15.1 %collective-permute-done.1.refs_3_ = bf16[2,8,64,512]{3,2,1,0:T(8,128)(2,1)} collective-permute-done((bf16[2,8,64,512]{3,2,1,0:T(8,128)(2,1)S(1)}, bf16[2,8,64,512]{3,2,1,0:T(8,128)(2,1)}, u32[]{:S(2)}, u32[]{:S(2)}) %collective-permute-start.1) | collective-permute-done | bytes 1048608 | tf_op jit(solution)/shard_map/ppermute | solution.py:393
  51.8 1.8 collective-permute-start.4
  53.7 11.4 %copy.32 = bf16[2,256,16,512]{3,1,0,2:T(8,128)(2,1)} copy(bf16[2,256,16,512]{3,2,1,0:T(8,128)(2,1)} %param.12) | data formatting | bytes 16777216 | tf_op args[3]
  65.1 2.1 gather_fusion
  67.2 0.8 maximum_maximum_fusion.1.refs_25_
  68.0 1.1 sine_convert_fusion.1
  69.2 0.9 maximum_maximum_fusion.refs_24_
  70.0 1.5 collective-permute-start.20
  71.5 1.5 collective-permute-start.2
  73.0 0.2 collective-permute-start.10
  73.3 1.1 slice.87
  74.3 2.1 collective-permute-done.4.refs_7_
  76.5 1.5 collective-permute-start.8
  78.0 1.1 slice.88
  79.0 1.1 slice.85
  80.1 13.6 %collective-permute-done.20.refs_1_ = bf16[128,2,16,128]{3,2,1,0:T(8,128)(2,1)S(1)} collective-permute-done((bf16[128,2,16,128]{3,2,1,0:T(8,128)(2,1)S(1)}, bf16[128,2,16,128]{3,2,1,0:T(8,128)(2,1)S(1)}, u32[]{:S(2)}, u32[]{:S(2)}) %collective-permute-start.20) | collective-permute-done | bytes 1048608 | tf_op jit(solution)/shard_map/ppermute | solution.py:393
  93.8 0.5 collective-permute-start.9
  94.3 1.5 collective-permute-start.6
  95.8 2.0 collective-permute-done.2.refs_5_
  97.8 0.5 collective-permute-start.15
  98.3 10.7 %collective-permute-done.8.refs_11_ = bf16[2,4,64,512]{3,2,1,0:T(8,128)(2,1)S(1)} collective-permute-done((bf16[2,4,64,512]{3,2,1,0:T(8,128)(2,1)S(1)}, bf16[2,4,64,512]{3,2,1,0:T(8,128)(2,1)S(1)}, u32[]{:S(2)}, u32[]{:S(2)}) %collective-permute-start.8) | collective-permute-done | bytes 524320 | tf_op jit(solution)/shard_map/ppermute | solution.py:397
  109.1 0.5 collective-permute-start.7
  109.6 10.2 %collective-permute-done.6.refs_9_ = bf16[2,4,64,512]{3,2,1,0:T(8,128)(2,1)S(1)} collective-permute-done((bf16[2,4,64,512]{3,2,1,0:T(8,128)(2,1)S(1)}, bf16[2,4,64,512]{3,2,1,0:T(8,128)(2,1)S(1)}, u32[]{:S(2)}, u32[]{:S(2)}) %collective-permute-start.6) | collective-permute-done | bytes 524320 | tf_op jit(solution)/shard_map/ppermute | solution.py:397
  119.8 3.7 %collective-permute-done.7.refs_10_ = bf16[2,4,64,512]{3,2,1,0:T(8,128)(2,1)S(1)} collective-permute-done((bf16[2,4,64,512]{3,2,1,0:T(8,128)(2,1)S(1)}, bf16[2,4,64,512]{3,2,1,0:T(8,128)(2,1)S(1)}, u32[]{:S(2)}, u32[]{:S(2)}) %collective-permute-start.7) | collective-permute-done | bytes 524320 | tf_op jit(solution)/shard_map/ppermute | solution.py:397
  123.5 0.5 collective-permute-start.19
  124.0 0.1 collective-permute-start.16
  124.1 0.5 collective-permute-start.17
  124.6 0.8 collective-permute-done.18.refs_21_
  125.4 0.7 collective-permute-done.19.refs_22_
  126.1 0.7 collective-permute-done.16.refs_19_
  126.9 0.7 collective-permute-done.17.refs_20_
  127.7 0.8 copy-done.24
  128.5 66.6 %shard_map.92 = bf16[256,2,16,128]{3,2,1,0:T(8,128)(2,1)} custom-call(s32[8]{0:T(128)} %copy-done.9, s32[256]{0:T(256)} %get-tuple-element.36.pos_ref, bf16[128,2,16,128]{3,2,1,0:T(8,128)(2,1)} %get-tuple-element.69.refs_0_, bf16[128,2,16,128]{3,2,1,0:T(8,128)(2,1)} %copy-done.10, bf16[2,128,64,512]{3,2,1,0:T(8,128)(2,1)} %refs_2_.1, ...), custom_call_target="tpu_custom_call" | custom-call | flops 25769803776 | bytes 111149056 | tf_op jit(solution)/shard_map/pallas_call | solution.py:318
  195.1 53.5 %all_to_all.15.weighted_ref = bf16[32,2,4,2,16,128]{5,4,3,2,1,0:T(8,128)(2,1)S(1)} all-to-all(bf16[32,2,4,2,16,128]{5,4,3,2,1,0:T(8,128)(2,1)} %bitcast.68), channel_id=1, replica_groups=mesh['mom'=2,'pts'=16] {'mom','pts'}, dimensions={0} | all-to-all | bytes 4194304 | tf_op jit(solution)/shard_map/all_to_all | solution.py:498
  248.7 51.4 %all_to_all.16 = bf16[32,4,2,32,128]{4,3,2,1,0:T(8,128)(2,1)S(1)} all-to-all(bf16[32,4,2,32,128]{4,3,2,1,0:T(8,128)(2,1)S(1)} %bitcast.67), channel_id=1, replica_groups=mesh['mom'=2,'pts'=16] {'mom','pts'}, dimensions={0} | all-to-all | bytes 4194304 | tf_op jit(solution)/shard_map/all_to_all | solution.py:484
  300.0 1.8 shard_map.93
  301.9 0.8 pad_maximum_fusion
  302.7 2.6 all-to-all-start.2
  305.3 0.1 copy.15
  305.5 1.4 dynamic-slice_convert_fusion
  306.9 14.3 %all-to-all-done.2 = bf16[32,4,2,8,128]{4,3,2,1,0:T(8,128)(2,1)S(1)} async-done(((bf16[32,4,2,8,128]{4,3,2,1,0:T(8,128)(2,1)}), bf16[32,4,2,8,128]{4,3,2,1,0:T(8,128)(2,1)S(1)}, u32[]{:S(2)}, u32[]{:S(2)}) %all-to-all-start.2) | async-done | bytes 524320 | tf_op jit(solution)/shard_map/all_to_all | solution.py:501
  321.2 1.0 gather_fusion.1
  322.2 0.1 convert_element_type.31
  322.4 0.2 fusion.29
  322.6 0.1 select_bitcast_fusion
  322.8 0.1 fusion
  322.9 0.5 copy-done.5
  323.4 0.2 fusion.4
  323.7 0.3 fusion.13
  324.0 0.1 maximum_bitcast_fusion.1
  324.1 0.1 maximum_bitcast_fusion.2
  324.2 1.2 maximum_bitcast_fusion
  (77 shorter events, 0.3 us)
Async XLA Ops:
  0.0 5.9 %copy-start.26 = (s32[8]{0:T(128)S(1)}, s32[8]{0:T(128)}, u32[]{:S(2)}) copy-start(s32[8]{0:T(128)} %constant.114.clone) | copy-start | bytes 100
  0.0 6.1 %copy-start.1 = (bf16[2,128,32,128]{3,2,1,0:T(8,128)(2,1)S(1)}, bf16[2,128,32,128]{3,2,1,0:T(8,128)(2,1)}, u32[]{:S(2)}) copy-start(bf16[2,128,32,128]{3,2,1,0:T(8,128)(2,1)} %cond_ref.1) | copy-start | bytes 6291460
  2.9 27.3 %collective-permute-start = (bf16[2,8,64,512]{3,2,1,0:T(8,128)(2,1)}, bf16[2,8,64,512]{3,2,1,0:T(8,128)(2,1)}, u32[]{:S(2)}, u32[]{:S(2)}) collective-permute-start(bf16[2,8,64,512]{3,2,1,0:T(8,128)(2,1)} %get-tuple-element.68), channel_id=1, source_target_pairs={{0,16},{16,0},{1,17},{17,1},{2,18},{18,2},{3,19},{19,3},{4,20},{20... | collective-permute-start | bytes 3145736 | tf_op jit(solution)/shard_map/ppermute | solution.py:393
  5.9 45.9 %collective-permute-start.1 = (bf16[2,8,64,512]{3,2,1,0:T(8,128)(2,1)S(1)}, bf16[2,8,64,512]{3,2,1,0:T(8,128)(2,1)}, u32[]{:S(2)}, u32[]{:S(2)}) collective-permute-start(bf16[2,8,64,512]{3,2,1,0:T(8,128)(2,1)S(1)} %get-tuple-element.67), channel_id=1, source_target_pairs={{0,16},{16,0},{1,17},{17,1},{2,18},{18,2},{3,19},{19,3},{4,20},{20... | collective-permute-start | bytes 3145736 | tf_op jit(solution)/shard_map/ppermute | solution.py:393
  5.9 12.2 %copy-start.9 = (s32[8]{0:T(128)}, s32[8]{0:T(128)S(1)}, u32[]{:S(2)}) copy-start(s32[8]{0:T(128)S(1)} %xor_multiply_fusion.base_ref) | copy-start | bytes 100
  6.1 3.4 %copy-start = (bf16[2,2,1,128,64,128]{5,4,3,2,1,0:T(8,128)(2,1)S(1)}, bf16[2,2,1,128,64,128]{5,4,3,2,1,0:T(8,128)(2,1)}, u32[]{:S(2)}) copy-start(bf16[2,2,1,128,64,128]{5,4,3,2,1,0:T(8,128)(2,1)} %amp_ref.1) | copy-start | bytes 25165828
  9.5 8.6 %copy-start.7 = (s32[256]{0:T(256)S(1)}, s32[256]{0:T(256)}, u32[]{:S(2)}) copy-start(s32[256]{0:T(256)} %param.15) | copy-start | bytes 3076
  30.2 41.3 %collective-permute-start.5 = (bf16[2,8,64,512]{3,2,1,0:T(8,128)(2,1)}, bf16[2,8,64,512]{3,2,1,0:T(8,128)(2,1)}, u32[]{:S(2)}, u32[]{:S(2)}) collective-permute-start(bf16[2,8,64,512]{3,2,1,0:T(8,128)(2,1)} %collective-permute-done.refs_4_), channel_id=1, source_target_pairs={{0,4},{1,5},{2,6},{3,7},{4,0},{5,1},{6,2},{7,3},{8,12},{9,13},{10,... | collective-permute-start | bytes 3145736 | tf_op jit(solution)/shard_map/ppermute | solution.py:397
  32.3 40.7 %collective-permute-start.3 = (bf16[2,8,64,512]{3,2,1,0:T(8,128)(2,1)}, bf16[2,8,64,512]{3,2,1,0:T(8,128)(2,1)}, u32[]{:S(2)}, u32[]{:S(2)}) collective-permute-start(bf16[2,8,64,512]{3,2,1,0:T(8,128)(2,1)} %collective-permute-done.refs_4_), channel_id=1, source_target_pairs={{0,2},{1,3},{2,0},{3,1},{4,6},{5,7},{6,4},{7,5},{8,10},{9,11},{10,... | collective-permute-start | bytes 3145736 | tf_op jit(solution)/shard_map/ppermute | solution.py:397
  51.8 24.6 %collective-permute-start.4 = (bf16[2,8,64,512]{3,2,1,0:T(8,128)(2,1)}, bf16[2,8,64,512]{3,2,1,0:T(8,128)(2,1)}, u32[]{:S(2)}, u32[]{:S(2)}) collective-permute-start(bf16[2,8,64,512]{3,2,1,0:T(8,128)(2,1)} %collective-permute-done.1.refs_3_), channel_id=1, source_target_pairs={{0,4},{1,5},{2,6},{3,7},{4,0},{5,1},{6,2},{7,3},{8,12},{9,13},{10,... | collective-permute-start | bytes 3145736 | tf_op jit(solution)/shard_map/ppermute | solution.py:397
  65.1 2.1 copy-start.4
  67.2 2.8 copy-start.3
  70.0 23.8 %collective-permute-start.20 = (bf16[128,2,16,128]{3,2,1,0:T(8,128)(2,1)S(1)}, bf16[128,2,16,128]{3,2,1,0:T(8,128)(2,1)S(1)}, u32[]{:S(2)}, u32[]{:S(2)}) collective-permute-start(bf16[128,2,16,128]{3,2,1,0:T(8,128)(2,1)S(1)} %copy-done.3), channel_id=1, source_target_pairs={{0,16},{16,0},{1,17},{17,1},{2,18},{18,2},{3,19},{19,3},{4,20},{20... | collective-permute-start | bytes 3145736 | tf_op jit(solution)/shard_map/ppermute | solution.py:393
  71.5 22.8 %collective-permute-start.11 = (bf16[2,8,64,512]{3,2,1,0:T(8,128)(2,1)}, bf16[2,8,64,512]{3,2,1,0:T(8,128)(2,1)S(1)}, u32[]{:S(2)}, u32[]{:S(2)}) collective-permute-start(bf16[2,8,64,512]{3,2,1,0:T(8,128)(2,1)} %collective-permute-done.refs_4_), channel_id=1, source_target_pairs={{0,1},{1,0},{2,3},{3,2},{4,5},{5,4},{6,7},{7,6},{8,9},{9,8},{10,11... | collective-permute-start | bytes 3145736 | tf_op jit(solution)/shard_map/ppermute | solution.py:397
  71.5 26.2 %collective-permute-start.2 = (bf16[2,8,64,512]{3,2,1,0:T(8,128)(2,1)}, bf16[2,8,64,512]{3,2,1,0:T(8,128)(2,1)S(1)}, u32[]{:S(2)}, u32[]{:S(2)}) collective-permute-start(bf16[2,8,64,512]{3,2,1,0:T(8,128)(2,1)} %collective-permute-done.1.refs_3_), channel_id=1, source_target_pairs={{0,2},{1,3},{2,0},{3,1},{4,6},{5,7},{6,4},{7,5},{8,10},{9,11},{10,... | collective-permute-start | bytes 3145736 | tf_op jit(solution)/shard_map/ppermute | solution.py:397
  73.0 24.7 %collective-permute-start.10 = (bf16[2,8,64,512]{3,2,1,0:T(8,128)(2,1)}, bf16[2,8,64,512]{3,2,1,0:T(8,128)(2,1)S(1)}, u32[]{:S(2)}, u32[]{:S(2)}) collective-permute-start(bf16[2,8,64,512]{3,2,1,0:T(8,128)(2,1)} %collective-permute-done.1.refs_3_), channel_id=1, source_target_pairs={{0,1},{1,0},{2,3},{3,2},{4,5},{5,4},{6,7},{7,6},{8,9},{9,8},{10,11... | collective-permute-start | bytes 3145736 | tf_op jit(solution)/shard_map/ppermute | solution.py:397
  76.5 32.5 %collective-permute-start.8 = (bf16[2,4,64,512]{3,2,1,0:T(8,128)(2,1)S(1)}, bf16[2,4,64,512]{3,2,1,0:T(8,128)(2,1)S(1)}, u32[]{:S(2)}, u32[]{:S(2)}) collective-permute-start(bf16[2,4,64,512]{3,2,1,0:T(8,128)(2,1)S(1)} %slice.87), channel_id=1, source_target_pairs={{0,2},{1,3},{2,0},{3,1},{4,6},{5,7},{6,4},{7,5},{8,10},{9,11},{10,... | collective-permute-start | bytes 1572872 | tf_op jit(solution)/shard_map/ppermute | solution.py:397
  93.8 30.3 %copy-start.10 = (bf16[128,2,16,128]{3,2,1,0:T(8,128)(2,1)}, bf16[128,2,16,128]{3,2,1,0:T(8,128)(2,1)S(1)}, u32[]{:S(2)}) copy-start(bf16[128,2,16,128]{3,2,1,0:T(8,128)(2,1)S(1)} %collective-permute-done.20.refs_1_) | copy-start | bytes 3145732
  93.8 15.3 %collective-permute-start.9 = (bf16[2,4,64,512]{3,2,1,0:T(8,128)(2,1)S(1)}, bf16[2,4,64,512]{3,2,1,0:T(8,128)(2,1)S(1)}, u32[]{:S(2)}, u32[]{:S(2)}) collective-permute-start(bf16[2,4,64,512]{3,2,1,0:T(8,128)(2,1)S(1)} %slice.88), channel_id=1, source_target_pairs={{0,4},{1,5},{2,6},{3,7},{4,0},{5,1},{6,2},{7,3},{8,12},{9,13},{10,... | collective-permute-start | bytes 1572872 | tf_op jit(solution)/shard_map/ppermute | solution.py:397
  94.3 30.3 %copy-start.11 = (bf16[2,8,64,512]{3,2,1,0:T(8,128)(2,1)}, bf16[2,8,64,512]{3,2,1,0:T(8,128)(2,1)S(1)}, u32[]{:S(2)}) copy-start(bf16[2,8,64,512]{3,2,1,0:T(8,128)(2,1)S(1)} %collective-permute-done.11.refs_14_) | copy-start | bytes 3145732
  94.3 25.5 %collective-permute-start.6 = (bf16[2,4,64,512]{3,2,1,0:T(8,128)(2,1)S(1)}, bf16[2,4,64,512]{3,2,1,0:T(8,128)(2,1)S(1)}, u32[]{:S(2)}, u32[]{:S(2)}) collective-permute-start(bf16[2,4,64,512]{3,2,1,0:T(8,128)(2,1)S(1)} %slice.85), channel_id=1, source_target_pairs={{0,2},{1,3},{2,0},{3,1},{4,6},{5,7},{6,4},{7,5},{8,10},{9,11},{10,... | collective-permute-start | bytes 1572872 | tf_op jit(solution)/shard_map/ppermute | solution.py:397
  97.8 30.7 %copy-start.6 = (bf16[2,8,64,512]{3,2,1,0:T(8,128)(2,1)}, bf16[2,8,64,512]{3,2,1,0:T(8,128)(2,1)S(1)}, u32[]{:S(2)}) copy-start(bf16[2,8,64,512]{3,2,1,0:T(8,128)(2,1)S(1)} %collective-permute-done.2.refs_5_) | copy-start | bytes 3145732
  97.8 25.7 %collective-permute-start.13 = (bf16[2,8,64,512]{3,2,1,0:T(8,128)(2,1)}, bf16[2,8,64,512]{3,2,1,0:T(8,128)(2,1)S(1)}, u32[]{:S(2)}, u32[]{:S(2)}) collective-permute-start(bf16[2,8,64,512]{3,2,1,0:T(8,128)(2,1)} %collective-permute-done.3.refs_6_), channel_id=1, source_target_pairs={{0,1},{1,0},{2,3},{3,2},{4,5},{5,4},{6,7},{7,6},{8,9},{9,8},{10,11... | collective-permute-start | bytes 3145736 | tf_op jit(solution)/shard_map/ppermute | solution.py:397
  97.8 26.8 %copy-start.12 = (bf16[2,8,64,512]{3,2,1,0:T(8,128)(2,1)}, bf16[2,8,64,512]{3,2,1,0:T(8,128)(2,1)S(1)}, u32[]{:S(2)}) copy-start(bf16[2,8,64,512]{3,2,1,0:T(8,128)(2,1)S(1)} %collective-permute-done.10.refs_13_) | copy-start | bytes 3145732
  97.8 26.2 %collective-permute-start.15 = (bf16[2,8,64,512]{3,2,1,0:T(8,128)(2,1)}, bf16[2,8,64,512]{3,2,1,0:T(8,128)(2,1)S(1)}, u32[]{:S(2)}, u32[]{:S(2)}) collective-permute-start(bf16[2,8,64,512]{3,2,1,0:T(8,128)(2,1)} %collective-permute-done.5.refs_8_), channel_id=1, source_target_pairs={{0,1},{1,0},{2,3},{3,2},{4,5},{5,4},{6,7},{7,6},{8,9},{9,8},{10,11... | collective-permute-start | bytes 3145736 | tf_op jit(solution)/shard_map/ppermute | solution.py:397
  109.0 19.5 %copy-start.17 = (bf16[2,4,64,512]{3,2,1,0:T(8,128)(2,1)}, bf16[2,4,64,512]{3,2,1,0:T(8,128)(2,1)S(1)}, u32[]{:S(2)}) copy-start(bf16[2,4,64,512]{3,2,1,0:T(8,128)(2,1)S(1)} %collective-permute-done.8.refs_11_) | copy-start | bytes 1572868
  109.0 15.1 %collective-permute-start.12 = (bf16[2,8,64,512]{3,2,1,0:T(8,128)(2,1)S(1)}, bf16[2,8,64,512]{3,2,1,0:T(8,128)(2,1)S(1)}, u32[]{:S(2)}, u32[]{:S(2)}) collective-permute-start(bf16[2,8,64,512]{3,2,1,0:T(8,128)(2,1)S(1)} %collective-permute-done.2.refs_5_), channel_id=1, source_target_pairs={{0,1},{1,0},{2,3},{3,2},{4,5},{5,4},{6,7},{7,6},{8,9},{9,8},{10,11... | collective-permute-start | bytes 3145736 | tf_op jit(solution)/shard_map/ppermute | solution.py:397
  109.0 18.6 %copy-start.18 = (bf16[2,4,64,512]{3,2,1,0:T(8,128)(2,1)}, bf16[2,4,64,512]{3,2,1,0:T(8,128)(2,1)S(1)}, u32[]{:S(2)}) copy-start(bf16[2,4,64,512]{3,2,1,0:T(8,128)(2,1)S(1)} %collective-permute-done.9.refs_12_) | copy-start | bytes 1572868
  109.1 14.4 %collective-permute-start.7 = (bf16[2,4,64,512]{3,2,1,0:T(8,128)(2,1)S(1)}, bf16[2,4,64,512]{3,2,1,0:T(8,128)(2,1)S(1)}, u32[]{:S(2)}, u32[]{:S(2)}) collective-permute-start(bf16[2,4,64,512]{3,2,1,0:T(8,128)(2,1)S(1)} %slice.86), channel_id=1, source_target_pairs={{0,4},{1,5},{2,6},{3,7},{4,0},{5,1},{6,2},{7,3},{8,12},{9,13},{10,... | collective-permute-start | bytes 1572872 | tf_op jit(solution)/shard_map/ppermute | solution.py:397
  119.8 7.9 %copy-start.19 = (bf16[2,4,64,512]{3,2,1,0:T(8,128)(2,1)}, bf16[2,4,64,512]{3,2,1,0:T(8,128)(2,1)S(1)}, u32[]{:S(2)}) copy-start(bf16[2,4,64,512]{3,2,1,0:T(8,128)(2,1)S(1)} %collective-permute-done.6.refs_9_) | copy-start | bytes 1572868
  119.8 4.8 %collective-permute-start.14 = (bf16[2,8,64,512]{3,2,1,0:T(8,128)(2,1)}, bf16[2,8,64,512]{3,2,1,0:T(8,128)(2,1)S(1)}, u32[]{:S(2)}, u32[]{:S(2)}) collective-permute-start(bf16[2,8,64,512]{3,2,1,0:T(8,128)(2,1)} %collective-permute-done.4.refs_7_), channel_id=1, source_target_pairs={{0,1},{1,0},{2,3},{3,2},{4,5},{5,4},{6,7},{7,6},{8,9},{9,8},{10,11... | collective-permute-start | bytes 3145736 | tf_op jit(solution)/shard_map/ppermute | solution.py:397
  123.5 4.2 %copy-start.20 = (bf16[2,4,64,512]{3,2,1,0:T(8,128)(2,1)}, bf16[2,4,64,512]{3,2,1,0:T(8,128)(2,1)S(1)}, u32[]{:S(2)}) copy-start(bf16[2,4,64,512]{3,2,1,0:T(8,128)(2,1)S(1)} %collective-permute-done.7.refs_10_) | copy-start | bytes 1572868
  123.5 1.9 collective-permute-start.18
  123.5 1.9 copy-start.13
  123.5 2.6 collective-permute-start.19
  124.0 2.1 copy-start.14
  124.0 2.9 collective-permute-start.16
  124.1 2.8 copy-start.15
  124.1 3.5 %collective-permute-start.17 = (bf16[2,4,64,512]{3,2,1,0:T(8,128)(2,1)S(1)}, bf16[2,4,64,512]{3,2,1,0:T(8,128)(2,1)S(1)}, u32[]{:S(2)}, u32[]{:S(2)}) collective-permute-start(bf16[2,4,64,512]{3,2,1,0:T(8,128)(2,1)S(1)} %collective-permute-done.7.refs_10_), channel_id=1, source_target_pairs={{0,1},{1,0},{2,3},{3,2},{4,5},{5,4},{6,7},{7,6},{8,9},{9,8},{10,11... | collective-permute-start | bytes 1572872 | tf_op jit(solution)/shard_map/ppermute | solution.py:397
  124.6 3.1 copy-start.16
  125.4 2.3 copy-start.21
  126.1 1.5 copy-start.22
  126.9 0.8 copy-start.23
  127.7 0.8 copy-start.24
  195.1 53.6 %copy-start.2 = (bf16[128,2,32,128]{3,2,1,0:T(8,128)(2,1)S(1)}, bf16[128,2,32,128]{3,2,1,0:T(8,128)(2,1)}, u32[]{:S(2)}) copy-start(bf16[128,2,32,128]{3,2,1,0:T(8,128)(2,1)} %gather_fusion) | copy-start | bytes 6291460
  300.0 5.3 %copy-start.8 = (f32[128,4]{0,1:T(4,128)S(1)}, f32[128,4]{0,1:T(4,128)}, u32[]{:S(2)}) copy-start(f32[128,4]{0,1:T(4,128)} %param.13) | copy-start | bytes 6148
  300.0 5.4 %copy-start.25 = (s32[128]{0:T(128)S(1)}, s32[128]{0:T(128)}, u32[]{:S(2)}) copy-start(s32[128]{0:T(128)} %param.16) | copy-start | bytes 1540
  302.7 18.5 %all-to-all-start.2 = ((bf16[32,4,2,8,128]{4,3,2,1,0:T(8,128)(2,1)}), bf16[32,4,2,8,128]{4,3,2,1,0:T(8,128)(2,1)S(1)}, u32[]{:S(2)}, u32[]{:S(2)}) async-start(bf16[32,4,2,8,128]{4,3,2,1,0:T(8,128)(2,1)} %pad_maximum_fusion), calls=%async_computation.2 | async-start | bytes 1048576 | tf_op jit(solution)/shard_map/all_to_all | solution.py:501
  322.6 0.8 copy-start.5
